TPU v7x, 256 devices: a whole 4x4x8 slice. The times are simulated.
256 devices in a mesh: sky: 32 (over z_lo, y, core), edge: 8 (over x, z_hi).
Axes of the slice: x: 4, y: 4, z: 8 (z_hi: 2, z_lo: 4; z = z_hi * 4 + z_lo), core: 2. Of those that a mesh axis runs over, the one named last changes fastest.
Arguments:
- node_feats: bfloat16 [131072, 128], P('sky'), may hold values from -6 to 6
- saved_agg: bfloat16 [131072, 128], P('sky'), may hold values from -9 to 9
- node_cot: bfloat16 [131072, 128], P('sky'), may hold values from -6 to 6
- edge_feats: bfloat16 [2097152, 128], P(('sky', 'edge')), may hold values from -6 to 6
- edge_cot: bfloat16 [2097152, 128], P(('sky', 'edge')), may hold values from -6 to 6
- senders: int32 [2097152], P(('sky', 'edge')), may hold values from 0 to 8191, as said below
- counts: int32 [131072], P('sky'), may hold values from 0 to 16, as said below
- send_lower: int32 [65536], P('sky'), may hold values from 0 to 4095, as said below
- send_upper: int32 [65536], P('sky'), may hold values from 0 to 4095, as said below
- w_recv: bfloat16 [128, 128], replicated, may hold values from -0.3125 to 0.3125
- w_send: bfloat16 [128, 128], replicated, may hold values from -0.3125 to 0.3125
- w_edge: bfloat16 [128, 128], replicated, may hold values from -0.3125 to 0.3125
- w_out: bfloat16 [128, 128], replicated, may hold values from -0.5 to 0.5
- b_edge: float32 [128], replicated, may hold values from -3 to 3
- v_self: bfloat16 [128, 128], replicated, may hold values from -0.375 to 0.375
- v_agg: bfloat16 [128, 128], replicated, may hold values from -0.375 to 0.375
- v_out: bfloat16 [128, 128], replicated, may hold values from -0.5 to 0.5
- b_node: float32 [128], replicated, may hold values from -3 to 3
Outputs:
- node_grad: bfloat16 [131072, 128], P('sky')
- edge_grad: bfloat16 [2097152, 128], P(('sky', 'edge'))
- edge_weight_grads: float32 [4, 128, 128], replicated
- node_weight_grads: float32 [3, 128, 128], replicated
- bias_grads: float32 [2, 128], replicated
Inputs may be any that keep to these rules, and one draw needn't show every extreme that they name: `senders`: A sender below 4096 is a node of the receiver's own tile; from 4096 up it is a halo slot of halo_rows. Dead slots name a sender too. `counts`: counts differ from tile to tile. `send_lower`: each tile's 2048 entries are distinct node rows of that tile. `send_upper`: each tile's 2048 entries are distinct node rows of that tile.
All inputs are finite; a program needn't handle non-finite values.
Results may differ from a plain program's by a relative error of at most 0.012.
Values may be sent and summed in bfloat16 or wider, within the bound.
A program may use at most 128 MiB of HBM per device.

v0:
```python
import jax
import jax.numpy as jnp
from jax import lax
from jax.sharding import PartitionSpec as P

DEGREE = 16


def passed_along(array, axis, by):
    size = lax.axis_size(axis)
    return lax.ppermute(array, axis, [(i, (i + by) % size) for i in range(size)])


def slope(z):
    s = jax.nn.sigmoid(z)
    return s * (1.0 + z * (1.0 - s))


def matmul(a, b):
    return jnp.dot(a, b, preferred_element_type=jnp.float32)


def outer_sum(a, b):
    return jnp.einsum("ef,eg->fg", a, b, preferred_element_type=jnp.float32)


def shards(
    node_feats,
    saved_agg,
    node_cot,
    edge_feats,
    edge_cot,
    senders,
    counts,
    send_lower,
    send_upper,
    w_recv,
    w_send,
    w_edge,
    w_out,
    b_edge,
    v_self,
    v_agg,
    v_out,
    b_node,
):
    nodes = node_feats.shape[0]
    width = node_feats.shape[1]
    halo = send_lower.shape[0]
    groups = lax.axis_size("edge")
    member = lax.axis_index("edge")
    share = nodes // groups
    start = member * share
    upper_rows = jnp.take(node_feats, send_upper, axis=0)
    lower_rows = jnp.take(node_feats, send_lower, axis=0)
    from_lower = passed_along(upper_rows, "sky", 1)
    from_upper = passed_along(lower_rows, "sky", -1)
    all_rows = jnp.concatenate([node_feats, from_lower, from_upper], axis=0)
    own = lax.dynamic_slice_in_dim(node_feats, start, share, 0)
    own_agg = lax.dynamic_slice_in_dim(saved_agg, start, share, 0)
    own_cot = lax.dynamic_slice_in_dim(node_cot, start, share, 0)
    own_counts = lax.dynamic_slice_in_dim(counts, start, share, 0)
    pre_node = matmul(own, v_self) + matmul(own_agg, v_agg) + b_node
    node_act = jax.nn.silu(pre_node).astype(jnp.bfloat16)
    d_pre_node = (matmul(own_cot, v_out.T) * slope(pre_node)).astype(jnp.bfloat16)
    d_agg = matmul(d_pre_node, v_agg.T).astype(jnp.bfloat16)
    d_node = own_cot.astype(jnp.float32) + matmul(d_pre_node, v_self.T)
    sender_rows = jnp.take(all_rows, senders, axis=0)
    pre_edge = (
        jnp.repeat(matmul(own, w_recv), DEGREE, axis=0)
        + matmul(sender_rows, w_send)
        + matmul(edge_feats, w_edge)
        + b_edge
    )
    hidden = jax.nn.silu(pre_edge).astype(jnp.bfloat16)
    live = (
        (jnp.arange(DEGREE, dtype=jnp.int32)[None, :] < own_counts[:, None])
        .astype(jnp.float32)
        .reshape(-1, 1)
    )
    d_msg = (
        (edge_cot.astype(jnp.float32) + jnp.repeat(d_agg.astype(jnp.float32), DEGREE, axis=0))
        * live
    ).astype(jnp.bfloat16)
    d_pre = (matmul(d_msg, w_out.T) * slope(pre_edge)).astype(jnp.bfloat16)
    edge_grad = matmul(d_pre, w_edge.T).astype(jnp.bfloat16)
    to_recv = matmul(d_pre, w_recv.T).reshape(share, DEGREE, width).sum(axis=1)
    to_send = jax.ops.segment_sum(matmul(d_pre, w_send.T), senders, num_segments=nodes + 2 * halo)
    local = to_send[:nodes]
    mine = lax.dynamic_slice_in_dim(local, start, share, 0) + d_node + to_recv
    local = lax.dynamic_update_slice_in_dim(local, mine, start, 0)
    cot_lower = to_send[nodes : nodes + halo]
    cot_upper = to_send[nodes + halo :]
    back_upper = passed_along(cot_lower.astype(jnp.bfloat16), "sky", -1).astype(cot_lower.dtype)
    back_lower = passed_along(cot_upper.astype(jnp.bfloat16), "sky", 1).astype(cot_upper.dtype)
    local = local.at[send_upper].add(back_upper).at[send_lower].add(back_lower)
    node_grad = lax.psum(local, "edge").astype(jnp.bfloat16)
    recv_grad = jnp.einsum(
        "nf,nkg->fg", own, d_pre.reshape(share, DEGREE, width), preferred_element_type=jnp.float32
    )
    edge_terms = jnp.stack(
        [
            recv_grad,
            outer_sum(sender_rows, d_pre),
            outer_sum(edge_feats, d_pre),
            outer_sum(hidden, d_msg),
        ]
    )
    node_terms = jnp.stack(
        [outer_sum(own, d_pre_node), outer_sum(own_agg, d_pre_node), outer_sum(node_act, own_cot)]
    )
    bias_terms = jnp.stack(
        [
            jnp.sum(d_pre.astype(jnp.float32), axis=0),
            jnp.sum(d_pre_node.astype(jnp.float32), axis=0),
        ]
    )
    edge_total, node_total, bias_total = lax.psum(
        (edge_terms, node_terms, bias_terms), ("sky", "edge")
    )
    scale = 1.0 / jnp.sqrt(jnp.float32(lax.axis_size("sky") * nodes * DEGREE))
    return (node_grad, edge_grad, edge_total * scale, node_total * scale, bias_total * scale)


def solution(mesh):
    in_specs = (
        P("sky", None),
        P("sky", None),
        P("sky", None),
        P(("sky", "edge"), None),
        P(("sky", "edge"), None),
        P(("sky", "edge")),
        P("sky"),
        P("sky"),
        P("sky"),
        P(),
        P(),
        P(),
        P(),
        P(),
        P(),
        P(),
        P(),
        P(),
    )
    out_specs = (P("sky", None), P(("sky", "edge"), None), P(), P(), P())
    return jax.shard_map(shards, mesh=mesh, in_specs=in_specs, out_specs=out_specs, check_vma=False)
```

profile of v0, /device:TPU:16, one launch (start us, length us, event | category | flops | bytes accessed | tf_op | source)
XLA Modules:
  0.0 639.3 jit_solution(5476758281294396873)
XLA Ops:
  7.2 0.0 copy-start
  7.2 0.0 all-reduce.4.cloned.1.call-start
  7.2 0.8 compare_and_fusion.1
  8.1 0.7 compare_select_fusion.1
  8.8 9.2 %gather_fusion.2 = bf16[2048,128]{1,0:T(8,128)(2,1)} fusion(bf16[4096,128]{1,0:T(8,128)(2,1)} %param.20, s32[2048]{0:T(1024)S(1)} %get-tuple-element.11), kind=kCustom, calls=%fused_computation.1.clone | custom fusion | bytes 1056768 | tf_op jit(solution)/shard_map/jit(_take)/gather | solution.py:55
  17.9 2.2 broadcast_select_fusion.3
  20.1 0.0 collective-permute-start.1
  20.1 0.6 compare_select_fusion.2
  20.7 8.1 %gather_fusion.1 = bf16[2048,128]{1,0:T(8,128)(2,1)} fusion(bf16[4096,128]{1,0:T(8,128)(2,1)S(1)} %copy-done.1, s32[2048]{0:T(1024)S(1)} %get-tuple-element.13), kind=kCustom, calls=%fused_computation.clone | custom fusion | bytes 1056768 | tf_op jit(solution)/shard_map/jit(_take)/gather | solution.py:54
  28.8 2.2 broadcast_select_fusion.4
  31.0 0.5 collective-permute-start
  31.5 0.2 fusion.27
  31.7 0.0 copy-start.14
  31.7 1.1 fusion.10
  32.8 0.0 copy-start.9
  32.8 1.8 convolution_bitcast_fusion
  34.6 1.7 convert_reduce_fusion.1
  36.3 1.7 convolution_bitcast_fusion.1
  38.0 0.9 convolution_bitcast_fusion.2
  38.8 0.2 fusion.12
  39.0 0.8 dynamic_slice.18
  39.8 0.8 fusion.18
  40.7 1.7 reshape.56
  42.4 0.0 copy-start.19
  42.4 3.7 fusion.3
  46.1 0.7 pad_maximum_fusion.2
  46.8 0.6 fusion.29
  47.4 0.2 fusion.25
  47.6 2.7 pad_maximum_fusion
  50.2 32.7 %gather_fusion = bf16[8192,128]{1,0:T(8,128)(2,1)} fusion(bf16[8192,128]{1,0:T(8,128)(2,1)} %pad_maximum_fusion, s32[8192]{0:T(1024)} %fusion.29), kind=kCustom, calls=%fused_computation.2 | custom fusion | bytes 4227072 | tf_op jit(solution)/shard_map/jit(_take)/gather | solution.py:68
  82.9 0.3 broadcast_in_dim.46
  83.2 1.3 copy-done.3
  84.5 2.7 convolution_add_fusion.1
  87.2 0.7 fusion
  87.9 0.9 copy-done.4
  88.8 1.9 fusion.13
  90.8 2.3 bitcast_reduce_fusion
  93.0 2.6 convolution_bitcast_fusion.4
  95.6 1.1 convert_reduce_fusion
  96.7 0.8 convolution_bitcast_fusion.3
  97.5 1.4 bitcast_reduce_fusion.1
  99.0 2.0 convolution_convert_fusion
  101.0 2.6 fusion.43
  103.6 46.7 %scatter_custom_fusion = f32[8192,128]{1,0:T(8,128)} fusion(s32[8192]{0:T(1024)} %param.25, f32[8192,128]{1,0:T(8,128)} %fusion.43, f32[]{:T(128)} %constant.18.clone.1), kind=kCustom, calls=%fused_computation.20 | custom fusion | flops 1048576 | bytes 4194816 | tf_op jit(solution)/shard_map/scatter-add | solution.py:88
  150.3 2.5 convert.6
  152.9 0.9 copy-done.2
  153.8 1.5 slice.20
  155.3 0.2 convolution_bitcast_fusion.5
  155.5 0.0 copy-start.22
  155.5 1.0 fusion.42
  156.6 1.1 collective-permute-start.3
  157.6 0.7 collective-permute-start.2
  158.3 0.7 pad_maximum_fusion.1
  159.0 0.0 all-reduce.4.cloned.1.call-update
  159.1 2.0 fusion.9
  161.1 83.2 %psum.31 = f32[2,128]{1,0:T(2,128)S(1)} all-reduce(f32[2,128]{1,0:T(2,128)S(1)} %pad_maximum_fusion.3), channel_id=1, replica_groups=mesh['sky'=32,'edge'=8] {'sky','edge'}, use_global_device_ids=true, to_apply=%region_10.12 | all-reduce | flops 256 | bytes 2048 | tf_op jit(solution)/shard_map/psum | solution.py:118
  244.2 0.6 broadcast_multiply_fusion.2
  244.8 176.2 %all-reduce.4.cloned.1.call-done = (f32[4,128,128]{2,1,0:T(8,128)}, f32[3,128,128]{2,1,0:T(8,128)}) async-done(((f32[4,128,128]{2,1,0:T(8,128)}, f32[3,128,128]{2,1,0:T(8,128)}), (f32[4,128,128]{2,1,0:T(8,128)}, f32[3,128,128]{2,1,0:T(8,128)})) %all-reduce.4.cloned.1.call-update) | async-done | bytes 458768 | tf_op jit(solution)/shard_map/psum | solution.py:118
  421.0 1.6 broadcast_multiply_fusion.1
  422.6 1.7 broadcast_multiply_fusion
  424.3 0.0 collective-permute-done.2
  424.3 13.4 %scatter_custom_fusion.1 = f32[4096,128]{1,0:T(8,128)} fusion(f32[4096,128]{1,0:T(8,128)} %fusion.9, s32[2048]{0:T(1024)} %get-tuple-element.12, bf16[2048,128]{1,0:T(8,128)(2,1)S(1)} %collective-permute-done.2), kind=kCustom, calls=%fused_computation.44 | custom fusion | flops 524288 | bytes 2621440 | tf_op jit(solution)/shard_map/scatter-add | solution.py:96
  437.7 13.3 %scatter_custom_fusion.2 = f32[4096,128]{1,0:T(8,128)} fusion(f32[4096,128]{1,0:T(8,128)} %scatter_custom_fusion.1, s32[2048]{0:T(1024)S(1)} %get-tuple-element.10, bf16[2048,128]{1,0:T(8,128)(2,1)S(1)} %collective-permute-done.3), kind=kCustom, calls=%fused_computation.42 | custom fusion | flops 524288 | bytes 2621440 | tf_op jit(solution)/shard_map/scatter-add | solution.py:96
  450.9 181.5 %all-reduce.5 = bf16[4096,128]{1,0:T(8,128)(2,1)} all-reduce(f32[4096,128]{1,0:T(8,128)} %scatter_custom_fusion.2), channel_id=1, replica_groups=mesh['sky'=32,'edge'=8] {'edge'}, use_global_device_ids=true, to_apply=%region_4.6 | all-reduce | flops 524288 | bytes 3145728 | tf_op jit(solution)/shard_map/psum | solution.py:97
  (50 shorter events, 0.1 us)
Async XLA Ops:
  7.2 80.0 %copy-start = (bf16[8192,128]{1,0:T(8,128)(2,1)S(1)}, bf16[8192,128]{1,0:T(8,128)(2,1)}, u32[]{:S(2)}) copy-start(bf16[8192,128]{1,0:T(8,128)(2,1)} %param.23) | copy-start | bytes 6291460
  7.2 413.8 %all-reduce.4.cloned.1.call-start = ((), (), s32[]{:S(2)}) async-start(), calls=%async_computation | async-start | bytes 917504 | tf_op jit(solution)/shard_map/psum | solution.py:118
  8.8 11.3 %copy-start.18 = (s32[2048]{0:T(1024)S(1)}, s32[2048]{0:T(1024)}, u32[]{:S(2)}) copy-start(s32[2048]{0:T(1024)} %param.28) | copy-start | bytes 24580
  8.8 12.0 %copy-start.1 = (bf16[4096,128]{1,0:T(8,128)(2,1)S(1)}, bf16[4096,128]{1,0:T(8,128)(2,1)}, u32[]{:S(2)}) copy-start(bf16[4096,128]{1,0:T(8,128)(2,1)} %param.20) | copy-start | bytes 3145732
  20.1 27.5 %collective-permute-start.1 = (bf16[2048,128]{1,0:T(8,128)(2,1)}, bf16[2048,128]{1,0:T(8,128)(2,1)}, u32[]{:S(2)}, u32[]{:S(2)}) collective-permute-start(bf16[2048,128]{1,0:T(8,128)(2,1)} %broadcast_select_fusion.3), channel_id=1, source_target_pairs={{0,248},{8,0},{16,8},{24,16},{32,24},{40,32},{48,40},{56,48},{64,5... | collective-permute-start | bytes 1572872 | tf_op jit(solution)/shard_map/ppermute | solution.py:11
  20.7 10.8 %copy-start.11 = (bf16[128,128]{1,0:T(8,128)(2,1)S(1)}, bf16[128,128]{1,0:T(8,128)(2,1)}, u32[]{:S(2)}) copy-start(bf16[128,128]{1,0:T(8,128)(2,1)} %param.34) | copy-start | bytes 98308
  20.7 10.9 %copy-start.13 = (bf16[128,128]{1,0:T(8,128)(2,1)S(1)}, bf16[128,128]{1,0:T(8,128)(2,1)}, u32[]{:S(2)}) copy-start(bf16[128,128]{1,0:T(8,128)(2,1)} %param.35) | copy-start | bytes 98308
  20.7 10.9 %copy-start.23 = (f32[128]{0:T(128)S(1)}, f32[128]{0:T(128)}, u32[]{:S(2)}) copy-start(f32[128]{0:T(128)} %param.37) | copy-start | bytes 1540
  28.8 5.8 copy-start.24
  31.0 16.6 %collective-permute-start = (bf16[2048,128]{1,0:T(8,128)(2,1)}, bf16[2048,128]{1,0:T(8,128)(2,1)}, u32[]{:S(2)}, u32[]{:S(2)}) collective-permute-start(bf16[2048,128]{1,0:T(8,128)(2,1)} %broadcast_select_fusion.4), channel_id=1, source_target_pairs={{0,8},{8,16},{16,24},{24,32},{32,40},{40,48},{48,56},{56,64},{64,7... | collective-permute-start | bytes 1572872 | tf_op jit(solution)/shard_map/ppermute | solution.py:11
  31.7 7.2 %copy-start.14 = (bf16[128,128]{1,0:T(8,128)(2,1)S(1)}, bf16[128,128]{1,0:T(8,128)(2,1)}, u32[]{:S(2)}) copy-start(bf16[128,128]{1,0:T(8,128)(2,1)} %param.35) | copy-start | bytes 98308
  32.8 7.0 %copy-start.9 = (s32[8192]{0:T(1024)S(1)}, s32[8192]{0:T(1024)}, u32[]{:S(2)}) copy-start(s32[8192]{0:T(1024)} %param.25) | copy-start | bytes 98308
  42.3 3.7 copy-start.5
  42.4 3.7 copy-start.6
  42.4 3.7 copy-start.15
  42.4 4.4 copy-start.10
  42.4 5.0 copy-start.19
  82.9 1.6 copy-start.3
  82.9 1.6 copy-start.8
  84.5 2.7 copy-start.7
  84.5 2.7 copy-start.21
  87.2 1.6 copy-start.4
  88.8 1.9 copy-start.25
  96.7 0.8 copy-start.20
  150.3 3.4 copy-start.2
  155.3 3.0 copy-start.16
  155.3 3.0 copy-start.17
  155.3 3.8 copy-start.12
  155.5 5.5 copy-start.22
  156.6 281.1 %collective-permute-start.3 = (bf16[2048,128]{1,0:T(8,128)(2,1)}, bf16[2048,128]{1,0:T(8,128)(2,1)S(1)}, u32[]{:S(2)}, u32[]{:S(2)}) collective-permute-start(bf16[2048,128]{1,0:T(8,128)(2,1)} %get-tuple-element.8), channel_id=1, source_target_pairs={{0,8},{8,16},{16,24},{24,32},{32,40},{40,48},{48,56},{56,64},{64,7... | collective-permute-start | bytes 1572872 | tf_op jit(solution)/shard_map/ppermute | solution.py:11
  157.6 266.6 %collective-permute-start.2 = (bf16[2048,128]{1,0:T(8,128)(2,1)}, bf16[2048,128]{1,0:T(8,128)(2,1)S(1)}, u32[]{:S(2)}, u32[]{:S(2)}) collective-permute-start(bf16[2048,128]{1,0:T(8,128)(2,1)} %get-tuple-element.9), channel_id=1, source_target_pairs={{0,248},{8,0},{16,8},{24,16},{32,24},{40,32},{48,40},{56,48},{64,5... | collective-permute-start | bytes 1572872 | tf_op jit(solution)/shard_map/ppermute | solution.py:11
Sparse Core Ops, SparseCore 0:
  159.2 261.7 all-reduce.3
where the time goes:
time: 641 us; the launch traced here: 639 us
  blocking collectives  265 us (41%)
  waiting for transfers between devices  176 us (27%)
  other arithmetic  96.6 us (15%)
  local copies, waits for them, and re-layouts  58.3 us (9%)
  matrix products  26.9 us (4%)
  between operations  14.3 us (2%)
    psum x1, blocking collectives, shards(): node_grad = lax.psum(local, 'edge').astype(jnp.bfloat16)  182 us
    psum x1, waiting for transfers between devices, shards(): lax.psum((edge_terms, node_terms, bias_terms), ('sky', 'edge'))  176 us
    psum x1, blocking collectives, shards(): lax.psum((edge_terms, node_terms, bias_terms), ('sky', 'edge'))  83.2 us
    scatter-add x1, other arithmetic, shards(): jax.ops.segment_sum(matmul(d_pre, w_send.T), senders, num_segments=nodes...  46.7 us
    gather x1, local copies, waits for them, and re-layouts, shards(): sender_rows = jnp.take(all_rows, senders, axis=0)  32.7 us
    scatter-add x2, other arithmetic, shards(): local = local.at[send_upper].add(back_upper).at[send_lower].add(back_lower)  26.7 us
    dot_general x12, matrix products, matmul(): return jnp.dot(a, b, preferred_element_type=jnp.float32)  16.9 us
  transfers between devices with their start and end apart: 5, of which 1 were waited for; matrix products, arithmetic and copies ran while one was open for 7% of the time, Pallas kernels for 0%

commit v1 on v0

--- a/solution.py
+++ b/solution.py
@@ -87,27 +87,13 @@
     to_recv = matmul(d_pre, w_recv.T).reshape(share, DEGREE, width).sum(axis=1)
     to_send = jax.ops.segment_sum(matmul(d_pre, w_send.T), senders, num_segments=nodes + 2 * halo)
     local = to_send[:nodes]
-    mine = lax.dynamic_slice_in_dim(local, start, share, 0) + d_node + to_recv
-    local = lax.dynamic_update_slice_in_dim(local, mine, start, 0)
     cot_lower = to_send[nodes : nodes + halo]
     cot_upper = to_send[nodes + halo :]
     back_upper = passed_along(cot_lower.astype(jnp.bfloat16), "sky", -1).astype(cot_lower.dtype)
     back_lower = passed_along(cot_upper.astype(jnp.bfloat16), "sky", 1).astype(cot_upper.dtype)
     local = local.at[send_upper].add(back_upper).at[send_lower].add(back_lower)
-    node_grad = lax.psum(local, "edge").astype(jnp.bfloat16)
     recv_grad = jnp.einsum(
         "nf,nkg->fg", own, d_pre.reshape(share, DEGREE, width), preferred_element_type=jnp.float32
-    )
-    edge_terms = jnp.stack(
-        [
-            recv_grad,
-            outer_sum(sender_rows, d_pre),
-            outer_sum(edge_feats, d_pre),
-            outer_sum(hidden, d_msg),
-        ]
-    )
-    node_terms = jnp.stack(
-        [outer_sum(own, d_pre_node), outer_sum(own_agg, d_pre_node), outer_sum(node_act, own_cot)]
     )
     bias_terms = jnp.stack(
         [
@@ -115,11 +101,35 @@
             jnp.sum(d_pre_node.astype(jnp.float32), axis=0),
         ]
     )
-    edge_total, node_total, bias_total = lax.psum(
-        (edge_terms, node_terms, bias_terms), ("sky", "edge")
+    terms = jnp.concatenate(
+        [
+            recv_grad,
+            outer_sum(sender_rows, d_pre),
+            outer_sum(edge_feats, d_pre),
+            outer_sum(hidden, d_msg),
+            outer_sum(own, d_pre_node),
+            outer_sum(own_agg, d_pre_node),
+            outer_sum(node_act, own_cot),
+            bias_terms,
+        ],
+        axis=0,
     )
+    used = terms.shape[0]
+    chunk = -(-used // (groups * 8)) * 8
+    terms = jnp.pad(terms, ((0, chunk * groups - used), (0, 0)))
+    terms = lax.psum(terms, "sky")
+    mine = lax.dynamic_slice_in_dim(local, start, share, 0) + d_node + to_recv
+    local = lax.dynamic_update_slice_in_dim(local, mine, start, 0)
+    summed = lax.psum(jnp.concatenate([local, terms], axis=0), "edge")
+    node_grad = summed[:nodes].astype(jnp.bfloat16)
+    totals = summed[nodes : nodes + used]
     scale = 1.0 / jnp.sqrt(jnp.float32(lax.axis_size("sky") * nodes * DEGREE))
-    return (node_grad, edge_grad, edge_total * scale, node_total * scale, bias_total * scale)
+    totals = totals * scale
+    blocks = width
+    edge_total = totals[: 4 * blocks].reshape(4, blocks, width)
+    node_total = totals[4 * blocks : 7 * blocks].reshape(3, blocks, width)
+    bias_total = totals[7 * blocks :]
+    return (node_grad, edge_grad, edge_total, node_total, bias_total)
 
 
 def solution(mesh):

time: 641 us -> 693 us (1.081)
  waiting for transfers between devices: 176 us -> 479 us
  blocking collectives: 265 us -> 0 us
  local copies, waits for them, and re-layouts: 58.3 us -> 68 us
    psum x1 -> x2, waiting for transfers between devices: 176 us -> 479 us  [the longest x1 246 us: shards(): terms = lax.psum(terms, 'sky')]
    psum x2 -> x0, blocking collectives: 265 us -> none  [the longest x1 182 us: shards(): node_grad = lax.psum(local, 'edge').astype(jnp.bfloat16)]
  transfers between devices with their start and end apart: 5 -> 6, of which waited for: 1 -> 2; matrix products, arithmetic and copies ran while one was open for 7% -> 10% of each run, Pallas kernels for 0% -> 0%
where the time goes in v1:
time: 693 us; the launch traced here: 690 us
  waiting for transfers between devices  479 us (69%)
  other arithmetic  97.3 us (14%)
  local copies, waits for them, and re-layouts  68 us (10%)
  matrix products  29.3 us (4%)
  between operations  14.4 us (2%)
    psum x1, waiting for transfers between devices, shards(): terms = lax.psum(terms, 'sky')  246 us
    psum x1, waiting for transfers between devices, shards(): summed = lax.psum(jnp.concatenate([local, terms], axis=0), 'edge')  234 us
    scatter-add x1, other arithmetic, shards(): jax.ops.segment_sum(matmul(d_pre, w_send.T), senders, num_segments=nodes...  46.5 us
    gather x1, local copies, waits for them, and re-layouts, shards(): sender_rows = jnp.take(all_rows, senders, axis=0)  32.8 us
    scatter-add x2, other arithmetic, shards(): local = local.at[send_upper].add(back_upper).at[send_lower].add(back_lower)  27.2 us
    dot_general x12, matrix products, matmul(): return jnp.dot(a, b, preferred_element_type=jnp.float32)  19.3 us
  transfers between devices with their start and end apart: 6, of which 2 were waited for; matrix products, arithmetic and copies ran while one was open for 10% of the time, Pallas kernels for 0%

profile of v1, /device:TPU:16, one launch (start us, length us, event | category | flops | bytes accessed | tf_op | source)
XLA Modules:
  0.0 690.1 jit_solution(3772573964208403021)
XLA Ops:
  7.2 0.0 copy-start
  7.2 0.0 all-reduce.4.cloned.1.call-start
  7.2 0.8 compare_select_fusion.1
  8.1 0.7 compare_and_fusion.1
  8.8 9.2 %gather_fusion.2 = bf16[2048,128]{1,0:T(8,128)(2,1)} fusion(bf16[4096,128]{1,0:T(8,128)(2,1)} %param.20, s32[2048]{0:T(1024)S(1)} %get-tuple-element.9), kind=kCustom, calls=%fused_computation.1.clone | custom fusion | bytes 1056768 | tf_op jit(solution)/shard_map/jit(_take)/gather | solution.py:55
  17.9 2.2 broadcast_select_fusion.3
  20.1 0.6 compare_select_fusion.2
  20.7 0.0 copy-start.17
  20.8 0.0 copy-start.23
  20.8 8.1 %gather_fusion.1 = bf16[2048,128]{1,0:T(8,128)(2,1)} fusion(bf16[4096,128]{1,0:T(8,128)(2,1)S(1)} %copy-done.1, s32[2048]{0:T(1024)S(1)} %get-tuple-element.11), kind=kCustom, calls=%fused_computation.clone | custom fusion | bytes 1056768 | tf_op jit(solution)/shard_map/jit(_take)/gather | solution.py:54
  28.8 2.2 broadcast_select_fusion.4
  31.0 0.5 collective-permute-start
  31.5 0.2 fusion.28
  31.7 1.1 fusion.7
  32.8 1.8 convert_reduce_fusion.1
  34.6 0.9 fusion.9
  35.5 0.9 fusion.22
  36.4 1.8 fusion.17
  38.1 1.4 fusion.30
  39.5 0.8 dynamic_slice.18
  40.3 0.8 fusion.15
  41.1 0.8 compare_and_fusion
  41.9 1.7 reshape.64
  43.6 3.5 fusion.3
  47.1 0.2 fusion.26
  47.3 1.8 fusion.16
  49.1 2.7 pad_maximum_fusion.1
  51.8 32.8 %gather_fusion = bf16[8192,128]{1,0:T(8,128)(2,1)} fusion(bf16[8192,128]{1,0:T(8,128)(2,1)} %pad_maximum_fusion.1, s32[8192]{0:T(1024)} %fusion.30), kind=kCustom, calls=%fused_computation.2 | custom fusion | bytes 4227072 | tf_op jit(solution)/shard_map/jit(_take)/gather | solution.py:68
  84.5 0.3 broadcast_in_dim.46
  84.8 1.3 copy-done.5
  86.1 2.7 convolution_add_fusion.1
  88.9 0.7 fusion
  89.6 0.9 copy-done.6
  90.4 2.9 bitcast_reduce_fusion
  93.4 2.6 fusion.14
  96.0 0.8 convolution_bitcast_fusion
  96.8 1.9 fusion.6
  98.7 2.7 fusion.44
  101.4 46.5 %scatter_custom_fusion = f32[8192,128]{1,0:T(8,128)} fusion(s32[8192]{0:T(1024)} %param.25, f32[8192,128]{1,0:T(8,128)} %fusion.44, f32[]{:T(128)} %constant.10.clone.1), kind=kCustom, calls=%fused_computation.22 | custom fusion | flops 1048576 | bytes 4194816 | tf_op jit(solution)/shard_map/scatter-add | solution.py:88
  147.8 2.4 convert.9
  150.3 1.1 fusion.43
  151.4 1.3 collective-permute-start.2
  152.6 1.1 convert_reduce_fusion
  153.7 0.2 fusion.24
  154.0 2.6 concatenate.10
  156.6 0.8 pad.4
  157.4 0.0 all-reduce.4.cloned.1.call-update
  157.4 0.0 all-reduce.6.cloned.1.call-start
  157.5 3.2 slice.41
  160.7 0.7 bitcast_reduce_fusion.1
  161.4 13.6 %scatter_custom_fusion.1 = f32[4096,128]{1,0:T(8,128)} fusion(f32[4096,128]{1,0:T(8,128)} %slice.41, s32[2048]{0:T(1024)} %get-tuple-element.10, bf16[2048,128]{1,0:T(8,128)(2,1)} %collective-permute-done.2), kind=kCustom, calls=%fused_computation.37 | custom fusion | flops 524288 | bytes 2621440 | tf_op jit(solution)/shard_map/scatter-add | solution.py:94
  175.1 13.6 %scatter_custom_fusion.2 = f32[4096,128]{1,0:T(8,128)} fusion(f32[4096,128]{1,0:T(8,128)} %scatter_custom_fusion.1, s32[2048]{0:T(1024)S(1)} %get-tuple-element.8, bf16[2048,128]{1,0:T(8,128)(2,1)} %collective-permute-done.3), kind=kCustom, calls=%fused_computation.35 | custom fusion | flops 524288 | bytes 2621440 | tf_op jit(solution)/shard_map/scatter-add | solution.py:94
  188.7 1.9 add_dynamic-update-slice_fusion
  190.6 245.6 %all-reduce.4.cloned.1.call-done = f32[960,128]{1,0:T(8,128)} async-done(((f32[960,128]{1,0:T(8,128)}), f32[960,128]{1,0:T(8,128)}) %all-reduce.4.cloned.1.call-update) | async-done | bytes 491536 | tf_op jit(solution)/shard_map/psum | solution.py:120
  436.1 3.4 pad_maximum_fusion
  439.6 0.0 all-reduce.6.cloned.1.call-update
  439.6 0.7 copy-done.13
  440.3 3.6 convolution_convert_fusion
  444.0 233.6 %all-reduce.6.cloned.1.call-done = f32[5056,128]{1,0:T(8,128)} async-done(((f32[5056,128]{1,0:T(8,128)}), f32[5056,128]{1,0:T(8,128)}) %all-reduce.6.cloned.1.call-update) | async-done | bytes 2588688 | tf_op jit(solution)/shard_map/psum | solution.py:123
  677.5 1.1 slice_multiply_fusion
  678.6 0.7 slice.46
  679.3 0.7 slice.47
  680.0 0.6 slice.48
  680.6 2.7 slice.51
  (53 shorter events, 0.1 us)
Async XLA Ops:
  7.2 81.6 %copy-start = (bf16[8192,128]{1,0:T(8,128)(2,1)S(1)}, bf16[8192,128]{1,0:T(8,128)(2,1)}, u32[]{:S(2)}) copy-start(bf16[8192,128]{1,0:T(8,128)(2,1)} %param.23) | copy-start | bytes 6291460
  7.2 429.0 %all-reduce.4.cloned.1.call-start = ((), (), s32[]{:S(2)}) async-start(), calls=%async_computation | async-start | bytes 983040 | tf_op jit(solution)/shard_map/psum | solution.py:120
  8.8 11.4 %copy-start.18 = (s32[2048]{0:T(1024)S(1)}, s32[2048]{0:T(1024)}, u32[]{:S(2)}) copy-start(s32[2048]{0:T(1024)} %param.28) | copy-start | bytes 24580
  8.8 12.0 %copy-start.1 = (bf16[4096,128]{1,0:T(8,128)(2,1)S(1)}, bf16[4096,128]{1,0:T(8,128)(2,1)}, u32[]{:S(2)}) copy-start(bf16[4096,128]{1,0:T(8,128)(2,1)} %param.20) | copy-start | bytes 3145732
  20.1 29.0 %collective-permute-start.1 = (bf16[2048,128]{1,0:T(8,128)(2,1)}, bf16[2048,128]{1,0:T(8,128)(2,1)}, u32[]{:S(2)}, u32[]{:S(2)}) collective-permute-start(bf16[2048,128]{1,0:T(8,128)(2,1)} %broadcast_select_fusion.3), channel_id=1, source_target_pairs={{0,248},{8,0},{16,8},{24,16},{32,24},{40,32},{48,40},{56,48},{64,5... | collective-permute-start | bytes 1572872 | tf_op jit(solution)/shard_map/ppermute | solution.py:11
  20.7 10.8 %copy-start.15 = (bf16[128,128]{1,0:T(8,128)(2,1)S(1)}, bf16[128,128]{1,0:T(8,128)(2,1)}, u32[]{:S(2)}) copy-start(bf16[128,128]{1,0:T(8,128)(2,1)} %param.34) | copy-start | bytes 98308
  20.7 10.9 %copy-start.17 = (bf16[128,128]{1,0:T(8,128)(2,1)S(1)}, bf16[128,128]{1,0:T(8,128)(2,1)}, u32[]{:S(2)}) copy-start(bf16[128,128]{1,0:T(8,128)(2,1)} %param.35) | copy-start | bytes 98308
  20.8 10.9 %copy-start.23 = (f32[128]{0:T(128)S(1)}, f32[128]{0:T(128)}, u32[]{:S(2)}) copy-start(f32[128]{0:T(128)} %param.37) | copy-start | bytes 1540
  28.8 4.0 copy-start.24
  31.0 18.1 %collective-permute-start = (bf16[2048,128]{1,0:T(8,128)(2,1)}, bf16[2048,128]{1,0:T(8,128)(2,1)}, u32[]{:S(2)}, u32[]{:S(2)}) collective-permute-start(bf16[2048,128]{1,0:T(8,128)(2,1)} %broadcast_select_fusion.4), channel_id=1, source_target_pairs={{0,8},{8,16},{16,24},{24,32},{32,40},{40,48},{48,56},{56,64},{64,7... | collective-permute-start | bytes 1572872 | tf_op jit(solution)/shard_map/ppermute | solution.py:11
  32.8 1.8 copy-start.9
  43.6 3.5 copy-start.19
  43.6 3.7 copy-start.10
  84.5 1.6 copy-start.5
  84.5 1.6 copy-start.11
  86.1 2.7 copy-start.12
  86.1 2.7 copy-start.21
  88.8 1.6 copy-start.6
  88.8 1.6 copy-start.25
  93.4 5.3 copy-start.2
  150.2 2.4 copy-start.3
  150.2 3.5 copy-start.14
  150.3 3.7 copy-start.7
  150.3 3.7 copy-start.8
  150.3 3.7 copy-start.22
  151.4 10.1 %collective-permute-start.2 = (bf16[2048,128]{1,0:T(8,128)(2,1)}, bf16[2048,128]{1,0:T(8,128)(2,1)}, u32[]{:S(2)}, u32[]{:S(2)}) collective-permute-start(bf16[2048,128]{1,0:T(8,128)(2,1)} %get-tuple-element.7), channel_id=1, source_target_pairs={{0,248},{8,0},{16,8},{24,16},{32,24},{40,32},{48,40},{56,48},{64,5... | collective-permute-start | bytes 1572872 | tf_op jit(solution)/shard_map/ppermute | solution.py:11
  152.6 22.4 %collective-permute-start.3 = (bf16[2048,128]{1,0:T(8,128)(2,1)}, bf16[2048,128]{1,0:T(8,128)(2,1)}, u32[]{:S(2)}, u32[]{:S(2)}) collective-permute-start(bf16[2048,128]{1,0:T(8,128)(2,1)} %get-tuple-element.6), channel_id=1, source_target_pairs={{0,8},{8,16},{16,24},{24,32},{32,40},{40,48},{48,56},{56,64},{64,7... | collective-permute-start | bytes 1572872 | tf_op jit(solution)/shard_map/ppermute | solution.py:11
  157.4 3.3 copy-start.20
  157.4 520.1 %all-reduce.6.cloned.1.call-start = ((), (), s32[]{:S(2)}) async-start(), calls=%async_computation.1 | async-start | bytes 5177344 | tf_op jit(solution)/shard_map/psum | solution.py:123
  157.5 3.2 copy-start.4
  161.4 27.2 %copy-start.16 = (bf16[128,128]{1,0:T(8,128)(2,1)S(1)}, bf16[128,128]{1,0:T(8,128)(2,1)}, u32[]{:S(2)}) copy-start(bf16[128,128]{1,0:T(8,128)(2,1)} %param.34) | copy-start | bytes 98308
  439.6 0.8 copy-start.13
Sparse Core Ops, SparseCore 0:
  157.5 278.5 all-reduce.3
  439.7 237.7 all-reduce.5

commit v2 on v1

--- a/solution.py
+++ b/solution.py
@@ -9,6 +9,41 @@
 def passed_along(array, axis, by):
     size = lax.axis_size(axis)
     return lax.ppermute(array, axis, [(i, (i + by) % size) for i in range(size)])
+
+
+EDGE_ORDER = (1, 2, 0)
+
+
+def exchanged(array, axis, bit):
+    size = lax.axis_size(axis)
+    return lax.ppermute(array, axis, [(i, i ^ (1 << bit)) for i in range(size)])
+
+
+def halving_sum(blocks, axis, me, order):
+    bits = len(order)
+    rest = blocks.shape[1:]
+    x = blocks.reshape((2,) * bits + rest)
+    axes = list(range(bits - 1, -1, -1))
+    for bit in order:
+        at = axes.index(bit)
+        keep = (me >> bit) & 1
+        mine = lax.dynamic_index_in_dim(x, keep, axis=at, keepdims=False)
+        other = lax.dynamic_index_in_dim(x, 1 - keep, axis=at, keepdims=False)
+        x = mine + exchanged(other, axis, bit)
+        axes.pop(at)
+    return x
+
+
+def doubling_gather(block, axis, me, order):
+    axes = []
+    for bit in reversed(order):
+        got = exchanged(block, axis, bit)
+        low = ((me >> bit) & 1) == 0
+        block = jnp.where(low, jnp.stack([block, got]), jnp.stack([got, block]))
+        axes.insert(0, bit)
+    bits = len(order)
+    block = jnp.transpose(block, [axes.index(b) for b in range(bits - 1, -1, -1)] + list(range(bits, block.ndim)))
+    return block.reshape((-1,) + block.shape[bits + 1 :])
 
 
 def slope(z):
@@ -117,12 +152,17 @@
     used = terms.shape[0]
     chunk = -(-used // (groups * 8)) * 8
     terms = jnp.pad(terms, ((0, chunk * groups - used), (0, 0)))
-    terms = lax.psum(terms, "sky")
     mine = lax.dynamic_slice_in_dim(local, start, share, 0) + d_node + to_recv
     local = lax.dynamic_update_slice_in_dim(local, mine, start, 0)
-    summed = lax.psum(jnp.concatenate([local, terms], axis=0), "edge")
-    node_grad = summed[:nodes].astype(jnp.bfloat16)
-    totals = summed[nodes : nodes + used]
+    packed = jnp.concatenate(
+        [local.reshape(groups, share, width), terms.reshape(groups, chunk, width)], axis=1
+    )
+    summed = halving_sum(packed, "edge", member, EDGE_ORDER)
+    node_grad = doubling_gather(summed[:share].astype(jnp.bfloat16), "edge", member, EDGE_ORDER)
+    totals = summed[share:]
+    for bit in range(lax.axis_size("sky").bit_length() - 1):
+        totals = totals + exchanged(totals, "sky", bit)
+    totals = doubling_gather(totals, "edge", member, EDGE_ORDER)[:used]
     scale = 1.0 / jnp.sqrt(jnp.float32(lax.axis_size("sky") * nodes * DEGREE))
     totals = totals * scale
     blocks = width

time: 693 us -> 325 us (0.47)
  waiting for transfers between devices: 479 us -> 83.5 us
  starting transfers between devices: 1.84 us -> 43.4 us
  between operations: 14.4 us -> 1.09 us
    psum x2 -> x0, waiting for transfers between devices: 479 us -> none  [the longest x1 246 us: shards(): terms = lax.psum(terms, 'sky')]
    ppermute x0 -> x14, waiting for transfers between devices: none -> 80 us  [exchanged(): return lax.ppermute(array, axis, [(i, i ^ 1 << bit) for i in range(size)])]
    ppermute x0 -> x14, starting transfers between devices: none -> 41.1 us  [exchanged(): return lax.ppermute(array, axis, [(i, i ^ 1 << bit) for i in range(size)])]
  transfers between devices with their start and end apart: 6 -> 18, of which waited for: 2 -> 11; matrix products, arithmetic and copies ran while one was open for 10% -> 16% of each run, Pallas kernels for 0% -> 0%
where the time goes in v2:
time: 325 us; the launch traced here: 322 us
  other arithmetic  101 us (31%)
  waiting for transfers between devices  83.5 us (26%)
  local copies, waits for them, and re-layouts  63 us (19%)
  starting transfers between devices  43.4 us (13%)
  matrix products  30.4 us (9%)
    ppermute x14, waiting for transfers between devices, exchanged(): return lax.ppermute(array, axis, [(i, i ^ 1 << bit) for i in range(size)])  80 us
    scatter-add x1, other arithmetic, shards(): jax.ops.segment_sum(matmul(d_pre, w_send.T), senders, num_segments=nodes...  46.5 us
    ppermute x14, starting transfers between devices, exchanged(): return lax.ppermute(array, axis, [(i, i ^ 1 << bit) for i in range(size)])  41.1 us
    gather x1, local copies, waits for them, and re-layouts, shards(): sender_rows = jnp.take(all_rows, senders, axis=0)  32.5 us
    scatter-add x2, other arithmetic, shards(): local = local.at[send_upper].add(back_upper).at[send_lower].add(back_lower)  27.2 us
    dot_general x12, matrix products, matmul(): return jnp.dot(a, b, preferred_element_type=jnp.float32)  20.4 us
    dot_general x6, matrix products, outer_sum(): return jnp.einsum('ef,eg->fg', a, b, preferred_element_type=jnp.float32)  9.79 us
    gather x1, local copies, waits for them, and re-layouts, shards(): lower_rows = jnp.take(node_feats, send_lower, axis=0)  9.16 us
  transfers between devices with their start and end apart: 18, of which 11 were waited for; matrix products, arithmetic and copies ran while one was open for 16% of the time, Pallas kernels for 0%

profile of v2, /device:TPU:16, one launch (start us, length us, event | category | flops | bytes accessed | tf_op | source)
XLA Modules:
  0.0 322.2 jit_solution(3406555835214708744)
XLA Ops:
  0.6 0.9 compare_and_fusion.1
  1.5 1.3 compare_select_fusion.1
  2.8 9.2 %gather_fusion.2 = bf16[2048,128]{1,0:T(8,128)(2,1)} fusion(bf16[4096,128]{1,0:T(8,128)(2,1)} %param.20, s32[2048]{0:T(1024)S(1)} %get-tuple-element.9), kind=kCustom, calls=%fused_computation.1.clone | custom fusion | bytes 1056768 | tf_op jit(solution)/shard_map/jit(_take)/gather | solution.py:90
  12.0 2.2 broadcast_select_fusion.3
  14.8 8.1 %gather_fusion.1 = bf16[2048,128]{1,0:T(8,128)(2,1)} fusion(bf16[4096,128]{1,0:T(8,128)(2,1)S(1)} %copy-done.1, s32[2048]{0:T(1024)S(1)} %get-tuple-element.11), kind=kCustom, calls=%fused_computation.clone | custom fusion | bytes 1056768 | tf_op jit(solution)/shard_map/jit(_take)/gather | solution.py:89
  22.8 2.2 broadcast_select_fusion.4
  25.7 1.1 fusion.12
  26.8 1.8 convert_reduce_fusion.1
  28.6 1.8 fusion.24
  30.3 0.9 fusion.29
  31.2 0.9 fusion.14
  32.9 1.4 fusion.37
  35.9 1.7 reshape.431
  37.6 3.6 %fusion.3 = bf16[8192,128]{1,0:T(8,128)(2,1)} fusion(bf16[8192,128]{1,0:T(8,128)(2,1)} %param.24, f32[8192]{0:T(1024)} %reshape.431, f32[512,128]{1,0:T(8,128)S(1)} %fusion.14), kind=kLoop, calls=%fused_computation.16 | loop fusion | flops 4194304 | bytes 4489216 | tf_op jit(solution)/shard_map/convert_element_type | solution.py:119
  41.4 1.8 fusion.23
  43.2 2.7 pad_maximum_fusion
  45.9 32.5 %gather_fusion = bf16[8192,128]{1,0:T(8,128)(2,1)} fusion(bf16[8192,128]{1,0:T(8,128)(2,1)} %pad_maximum_fusion, s32[8192]{0:T(1024)} %fusion.37), kind=kCustom, calls=%fused_computation.2 | custom fusion | bytes 4227072 | tf_op jit(solution)/shard_map/jit(_take)/gather | solution.py:103
  78.7 1.3 copy-done.5
  80.0 2.7 convolution_add_fusion.1
  83.5 0.8 copy-done.8
  84.3 1.9 fusion.6
  86.2 2.3 bitcast_reduce_fusion
  88.5 2.6 fusion.20
  91.2 1.1 convert_reduce_fusion
  92.3 2.7 fusion.51
  94.9 46.5 %scatter_custom_fusion = f32[8192,128]{1,0:T(8,128)} fusion(s32[8192]{0:T(1024)} %param.25, f32[8192,128]{1,0:T(8,128)} %fusion.51, f32[]{:T(128)} %constant.51.clone.1), kind=kCustom, calls=%fused_computation.24 | custom fusion | flops 1048576 | bytes 4194816 | tf_op jit(solution)/shard_map/scatter-add | solution.py:123
  141.5 2.5 convert.9
  144.0 0.9 copy-done.4
  144.9 1.5 slice.45
  146.6 1.1 fusion.50
  147.7 1.1 collective-permute-start.3
  150.5 2.5 bitcast_reduce_fusion.1
  153.0 3.5 %collective-permute-done.2 = bf16[2048,128]{1,0:T(8,128)(2,1)} collective-permute-done((bf16[2048,128]{1,0:T(8,128)(2,1)}, bf16[2048,128]{1,0:T(8,128)(2,1)}, u32[]{:S(2)}, u32[]{:S(2)}) %collective-permute-start.2) | collective-permute-done | bytes 524320 | tf_op jit(solution)/shard_map/ppermute | solution.py:11
  156.5 13.6 %scatter_custom_fusion.1 = f32[4096,128]{1,0:T(8,128)} fusion(f32[4096,128]{1,0:T(8,128)} %slice.45, s32[2048]{0:T(1024)} %get-tuple-element.10, bf16[2048,128]{1,0:T(8,128)(2,1)} %collective-permute-done.2), kind=kCustom, calls=%fused_computation.46 | custom fusion | flops 524288 | bytes 2621440 | tf_op jit(solution)/shard_map/scatter-add | solution.py:129
  170.2 13.6 %scatter_custom_fusion.2 = f32[4096,128]{1,0:T(8,128)} fusion(f32[4096,128]{1,0:T(8,128)} %scatter_custom_fusion.1, s32[2048]{0:T(1024)} %get-tuple-element.8, bf16[2048,128]{1,0:T(8,128)(2,1)} %collective-permute-done.3), kind=kCustom, calls=%fused_computation.44 | custom fusion | flops 524288 | bytes 2621440 | tf_op jit(solution)/shard_map/scatter-add | solution.py:129
  183.8 1.9 add_dynamic-update-slice_fusion
  185.7 2.4 fusion.8
  188.0 1.5 collective-permute-start.4
  189.5 28.1 %collective-permute-done.4 = f32[2,2,632,128]{3,2,1,0:T(8,128)} collective-permute-done((f32[2,2,632,128]{3,2,1,0:T(8,128)}, f32[2,2,632,128]{3,2,1,0:T(8,128)}, u32[]{:S(2)}, u32[]{:S(2)}) %collective-permute-start.4) | collective-permute-done | bytes 1294368 | tf_op jit(solution)/shard_map/ppermute | solution.py:19
  217.6 1.8 fusion.11
  219.4 0.9 dynamic-slice_bitcast_fusion
  220.3 3.0 collective-permute-start.5
  223.3 15.3 %collective-permute-done.5 = f32[2,632,128]{2,1,0:T(8,128)} collective-permute-done((f32[2,632,128]{2,1,0:T(8,128)}, f32[2,632,128]{2,1,0:T(8,128)}, u32[]{:S(2)}, u32[]{:S(2)}) %collective-permute-start.5) | collective-permute-done | bytes 647200 | tf_op jit(solution)/shard_map/ppermute | solution.py:19
  238.6 1.2 bitcast_add_fusion.1
  240.6 7.3 %collective-permute-start.6 = (f32[632,128]{1,0:T(8,128)S(1)}, f32[632,128]{1,0:T(8,128)S(1)}, u32[]{:S(2)}, u32[]{:S(2)}) collective-permute-start(f32[632,128]{1,0:T(8,128)S(1)} %dynamic-slice_bitcast_fusion.1), channel_id=1, source_target_pairs={{0,1},{1,0},{2,3},{3,2},{4,5},{5,4},{6,7},{7,6},{8,9},{9,8},{10,11... | collective-permute-start | bytes 970760 | tf_op jit(solution)/shard_map/ppermute | solution.py:19
  247.9 9.5 %collective-permute-done.6 = f32[632,128]{1,0:T(8,128)S(1)} collective-permute-done((f32[632,128]{1,0:T(8,128)S(1)}, f32[632,128]{1,0:T(8,128)S(1)}, u32[]{:S(2)}, u32[]{:S(2)}) %collective-permute-start.6) | collective-permute-done | bytes 323616 | tf_op jit(solution)/shard_map/ppermute | solution.py:19
  257.4 1.0 bitcast_add_fusion.2
  258.5 3.6 %convolution_convert_fusion = bf16[8192,128]{1,0:T(8,128)(2,1)} fusion(bf16[8192,128]{1,0:T(8,128)(2,1)} %copy-done.2, bf16[128,128]{1,0:T(8,128)(2,1)S(1)} %copy-done.14), kind=kOutput, calls=%fused_computation.11 | convolution fusion | flops 269484032 | bytes 4227072 | tf_op jit(solution)/shard_map/dot_general | solution.py:55
  262.2 5.9 %collective-permute-start.11 = (f32[120,128]{1,0:T(8,128)S(1)}, f32[120,128]{1,0:T(8,128)S(1)}, u32[]{:S(2)}, u32[]{:S(2)}) collective-permute-start(f32[120,128]{1,0:T(8,128)S(1)} %slice_add_fusion), channel_id=1, source_target_pairs={{0,16},{8,24},{16,0},{24,8},{32,48},{40,56},{48,32},{56,40},{64,80... | collective-permute-start | bytes 184328 | tf_op jit(solution)/shard_map/ppermute | solution.py:19
  268.1 6.2 %collective-permute-start.7 = (bf16[512,128]{1,0:T(8,128)(2,1)S(1)}, bf16[512,128]{1,0:T(8,128)(2,1)S(1)}, u32[]{:S(2)}, u32[]{:S(2)}) collective-permute-start(bf16[512,128]{1,0:T(8,128)(2,1)S(1)} %slice.57), channel_id=1, source_target_pairs={{0,1},{1,0},{2,3},{3,2},{4,5},{5,4},{6,7},{7,6},{8,9},{9,8},{10,11... | collective-permute-start | bytes 393224 | tf_op jit(solution)/shard_map/ppermute | solution.py:19
  274.4 2.2 collective-permute-start.12
  276.5 3.9 %collective-permute-done.12 = f32[120,128]{1,0:T(8,128)S(1)} collective-permute-done((f32[120,128]{1,0:T(8,128)S(1)}, f32[120,128]{1,0:T(8,128)S(1)}, u32[]{:S(2)}, u32[]{:S(2)}) %collective-permute-start.12) | collective-permute-done | bytes 61472 | tf_op jit(solution)/shard_map/ppermute | solution.py:19
  280.4 1.1 collective-permute-start.13
  281.5 3.1 collective-permute-start.8
  284.8 1.5 collective-permute-start.14
  286.3 4.3 %collective-permute-done.14 = f32[120,128]{1,0:T(8,128)S(1)} collective-permute-done((f32[120,128]{1,0:T(8,128)S(1)}, f32[120,128]{1,0:T(8,128)S(1)}, u32[]{:S(2)}, u32[]{:S(2)}) %collective-permute-start.14) | collective-permute-done | bytes 61472 | tf_op jit(solution)/shard_map/ppermute | solution.py:19
  290.6 4.1 %collective-permute-start.15 = (f32[120,128]{1,0:T(8,128)S(1)}, f32[120,128]{1,0:T(8,128)S(1)}, u32[]{:S(2)}, u32[]{:S(2)}) collective-permute-start(f32[120,128]{1,0:T(8,128)S(1)} %add.170), channel_id=1, source_target_pairs={{0,1},{1,0},{2,3},{3,2},{4,5},{5,4},{6,7},{7,6},{8,9},{9,8},{10,11... | collective-permute-start | bytes 184328 | tf_op jit(solution)/shard_map/ppermute | solution.py:19
  294.8 4.3 %collective-permute-done.15 = f32[120,128]{1,0:T(8,128)S(1)} collective-permute-done((f32[120,128]{1,0:T(8,128)S(1)}, f32[120,128]{1,0:T(8,128)S(1)}, u32[]{:S(2)}, u32[]{:S(2)}) %collective-permute-start.15) | collective-permute-done | bytes 61472 | tf_op jit(solution)/shard_map/ppermute | solution.py:19
  299.1 2.9 collective-permute-start.16
  302.0 4.8 %collective-permute-done.16 = f32[2,120,128]{2,1,0:T(8,128)S(1)} collective-permute-done((f32[2,120,128]{2,1,0:T(8,128)S(1)}, f32[2,120,128]{2,1,0:T(8,128)S(1)}, u32[]{:S(2)}, u32[]{:S(2)}) %collective-permute-start.16) | collective-permute-done | bytes 122912 | tf_op jit(solution)/shard_map/ppermute | solution.py:19
  306.9 1.4 collective-permute-start.17
  309.3 6.1 %collective-permute-done.17 = f32[2,2,120,128]{3,2,1,0:T(8,128)S(1)} collective-permute-done((f32[2,2,120,128]{3,2,1,0:T(8,128)S(1)}, f32[2,2,120,128]{3,2,1,0:T(8,128)S(1)}, u32[]{:S(2)}, u32[]{:S(2)}) %collective-permute-start.17) | collective-permute-done | bytes 245792 | tf_op jit(solution)/shard_map/ppermute | solution.py:19
  317.4 3.5 %collective-permute-done.9 = bf16[2,2,512,128]{3,2,1,0:T(8,128)(2,1)S(1)} collective-permute-done((bf16[2,2,512,128]{3,2,1,0:T(8,128)(2,1)S(1)}, bf16[2,2,512,128]{3,2,1,0:T(8,128)(2,1)S(1)}, u32[]{:S(2)}, u32[]{:S(2)}) %collective-permute-start.9) | collective-permute-done | bytes 524320 | tf_op jit(solution)/shard_map/ppermute | solution.py:19
  321.1 1.0 copy.26
  (111 shorter events, 11.3 us)
Async XLA Ops:
  0.6 82.1 %copy-start = (bf16[8192,128]{1,0:T(8,128)(2,1)S(1)}, bf16[8192,128]{1,0:T(8,128)(2,1)}, u32[]{:S(2)}) copy-start(bf16[8192,128]{1,0:T(8,128)(2,1)} %param.23) | copy-start | bytes 6291460
  2.8 11.3 %copy-start.23 = (s32[2048]{0:T(1024)S(1)}, s32[2048]{0:T(1024)}, u32[]{:S(2)}) copy-start(s32[2048]{0:T(1024)} %param.28) | copy-start | bytes 24580
  2.8 12.0 %copy-start.1 = (bf16[4096,128]{1,0:T(8,128)(2,1)S(1)}, bf16[4096,128]{1,0:T(8,128)(2,1)}, u32[]{:S(2)}) copy-start(bf16[4096,128]{1,0:T(8,128)(2,1)} %param.20) | copy-start | bytes 3145732
  14.1 29.1 %collective-permute-start.1 = (bf16[2048,128]{1,0:T(8,128)(2,1)}, bf16[2048,128]{1,0:T(8,128)(2,1)}, u32[]{:S(2)}, u32[]{:S(2)}) collective-permute-start(bf16[2048,128]{1,0:T(8,128)(2,1)} %broadcast_select_fusion.3), channel_id=1, source_target_pairs={{0,248},{8,0},{16,8},{24,16},{32,24},{40,32},{48,40},{56,48},{64,5... | collective-permute-start | bytes 1572872 | tf_op jit(solution)/shard_map/ppermute | solution.py:11
  14.8 10.8 %copy-start.15 = (bf16[128,128]{1,0:T(8,128)(2,1)S(1)}, bf16[128,128]{1,0:T(8,128)(2,1)}, u32[]{:S(2)}) copy-start(bf16[128,128]{1,0:T(8,128)(2,1)} %param.34) | copy-start | bytes 98308
  14.8 10.9 %copy-start.17 = (bf16[128,128]{1,0:T(8,128)(2,1)S(1)}, bf16[128,128]{1,0:T(8,128)(2,1)}, u32[]{:S(2)}) copy-start(bf16[128,128]{1,0:T(8,128)(2,1)} %param.35) | copy-start | bytes 98308
  14.8 10.9 %copy-start.28 = (f32[128]{0:T(128)S(1)}, f32[128]{0:T(128)}, u32[]{:S(2)}) copy-start(f32[128]{0:T(128)} %param.37) | copy-start | bytes 1540
  22.8 4.0 %copy-start.29 = (bf16[128,128]{1,0:T(8,128)(2,1)S(1)}, bf16[128,128]{1,0:T(8,128)(2,1)}, u32[]{:S(2)}) copy-start(bf16[128,128]{1,0:T(8,128)(2,1)} %param.36) | copy-start | bytes 98308
  25.0 18.2 %collective-permute-start = (bf16[2048,128]{1,0:T(8,128)(2,1)}, bf16[2048,128]{1,0:T(8,128)(2,1)}, u32[]{:S(2)}, u32[]{:S(2)}) collective-permute-start(bf16[2048,128]{1,0:T(8,128)(2,1)} %broadcast_select_fusion.4), channel_id=1, source_target_pairs={{0,8},{8,16},{16,24},{24,32},{32,40},{40,48},{48,56},{56,64},{64,7... | collective-permute-start | bytes 1572872 | tf_op jit(solution)/shard_map/ppermute | solution.py:11
  26.8 3.5 %copy-start.11 = (f32[512,128]{1,0:T(8,128)}, f32[512,128]{1,0:T(8,128)S(1)}, u32[]{:S(2)}) copy-start(f32[512,128]{1,0:T(8,128)S(1)} %fusion.12) | copy-start | bytes 786436
  35.9 42.8 %copy-start.18 = (pred[8192]{0:T(1024)(128)(4,1)}, pred[8192]{0:T(1024)(128)(4,1)S(1)}, u32[]{:S(2)}) copy-start(pred[8192]{0:T(1024)(128)(4,1)S(1)} %compare_and_fusion) | copy-start | bytes 24580
  37.6 3.6 %copy-start.24 = (bf16[128,128]{1,0:T(8,128)(2,1)S(1)}, bf16[128,128]{1,0:T(8,128)(2,1)}, u32[]{:S(2)}) copy-start(bf16[128,128]{1,0:T(8,128)(2,1)} %param.29) | copy-start | bytes 98308
  37.6 3.8 %copy-start.12 = (f32[512,128]{1,0:T(8,128)S(1)}, f32[512,128]{1,0:T(8,128)}, u32[]{:S(2)}) copy-start(f32[512,128]{1,0:T(8,128)} %copy-done.11) | copy-start | bytes 786436
  78.4 1.6 copy-start.5
  78.4 1.6 copy-start.13
  80.0 2.7 copy-start.14
  80.0 2.7 copy-start.26
  82.7 1.6 copy-start.8
  84.3 1.9 copy-start.30
  86.2 2.3 copy-start.19
  88.5 3.7 %copy-start.2 = (bf16[8192,128]{1,0:T(8,128)(2,1)}, bf16[8192,128]{1,0:T(8,128)(2,1)S(1)}, u32[]{:S(2)}) copy-start(bf16[8192,128]{1,0:T(8,128)(2,1)S(1)} %get-tuple-element.13) | copy-start | bytes 6291460
  141.5 3.4 %copy-start.4 = (f32[8192,128]{1,0:T(8,128)S(1)}, f32[8192,128]{1,0:T(8,128)}, u32[]{:S(2)}) copy-start(f32[8192,128]{1,0:T(8,128)} %scatter_custom_fusion) | copy-start | bytes 12582916
  146.4 3.2 copy-start.3
  147.7 22.5 %collective-permute-start.3 = (bf16[2048,128]{1,0:T(8,128)(2,1)}, bf16[2048,128]{1,0:T(8,128)(2,1)}, u32[]{:S(2)}, u32[]{:S(2)}) collective-permute-start(bf16[2048,128]{1,0:T(8,128)(2,1)} %get-tuple-element.6), channel_id=1, source_target_pairs={{0,8},{8,16},{16,24},{24,32},{32,40},{40,48},{48,56},{56,64},{64,7... | collective-permute-start | bytes 1572872 | tf_op jit(solution)/shard_map/ppermute | solution.py:11
  148.7 1.6 copy-start.9
  148.7 1.6 copy-start.10
  148.7 1.6 copy-start.20
  148.7 1.6 copy-start.21
  148.7 1.6 copy-start.22
  148.8 1.6 copy-start.27
  148.8 1.7 copy-start.25
  148.8 7.8 %collective-permute-start.2 = (bf16[2048,128]{1,0:T(8,128)(2,1)}, bf16[2048,128]{1,0:T(8,128)(2,1)}, u32[]{:S(2)}, u32[]{:S(2)}) collective-permute-start(bf16[2048,128]{1,0:T(8,128)(2,1)} %get-tuple-element.7), channel_id=1, source_target_pairs={{0,248},{8,0},{16,8},{24,16},{32,24},{40,32},{48,40},{56,48},{64,5... | collective-permute-start | bytes 1572872 | tf_op jit(solution)/shard_map/ppermute | solution.py:11
  150.5 35.1 %copy-start.6 = (f32[960,128]{1,0:T(8,128)}, f32[960,128]{1,0:T(8,128)S(1)}, u32[]{:S(2)}) copy-start(f32[960,128]{1,0:T(8,128)S(1)} %pad.4) | copy-start | bytes 1474564
  156.5 27.2 %copy-start.16 = (bf16[128,128]{1,0:T(8,128)(2,1)S(1)}, bf16[128,128]{1,0:T(8,128)(2,1)}, u32[]{:S(2)}) copy-start(bf16[128,128]{1,0:T(8,128)(2,1)} %param.34) | copy-start | bytes 98308
  188.0 29.6 %collective-permute-start.4 = (f32[2,2,632,128]{3,2,1,0:T(8,128)}, f32[2,2,632,128]{3,2,1,0:T(8,128)}, u32[]{:S(2)}, u32[]{:S(2)}) collective-permute-start(f32[2,2,632,128]{3,2,1,0:T(8,128)} %fusion.8), channel_id=1, source_target_pairs={{0,2},{1,3},{2,0},{3,1},{4,6},{5,7},{6,4},{7,5},{8,10},{9,11},{10,... | collective-permute-start | bytes 3883016 | tf_op jit(solution)/shard_map/ppermute | solution.py:19
  220.3 18.4 %collective-permute-start.5 = (f32[2,632,128]{2,1,0:T(8,128)}, f32[2,632,128]{2,1,0:T(8,128)}, u32[]{:S(2)}, u32[]{:S(2)}) collective-permute-start(f32[2,632,128]{2,1,0:T(8,128)} %dynamic-slice_bitcast_fusion), channel_id=1, source_target_pairs={{0,4},{1,5},{2,6},{3,7},{4,0},{5,1},{6,2},{7,3},{8,12},{9,13},{10,... | collective-permute-start | bytes 1941512 | tf_op jit(solution)/shard_map/ppermute | solution.py:19
  239.8 0.8 copy-start.7
  240.6 16.8 %collective-permute-start.6 = (f32[632,128]{1,0:T(8,128)S(1)}, f32[632,128]{1,0:T(8,128)S(1)}, u32[]{:S(2)}, u32[]{:S(2)}) collective-permute-start(f32[632,128]{1,0:T(8,128)S(1)} %dynamic-slice_bitcast_fusion.1), channel_id=1, source_target_pairs={{0,1},{1,0},{2,3},{3,2},{4,5},{5,4},{6,7},{7,6},{8,9},{9,8},{10,11... | collective-permute-start | bytes 970760 | tf_op jit(solution)/shard_map/ppermute | solution.py:19
  258.4 3.7 %collective-permute-start.10 = (f32[120,128]{1,0:T(8,128)S(1)}, f32[120,128]{1,0:T(8,128)S(1)}, u32[]{:S(2)}, u32[]{:S(2)}) collective-permute-start(f32[120,128]{1,0:T(8,128)S(1)} %slice.49), channel_id=1, source_target_pairs={{0,8},{8,0},{16,24},{24,16},{32,40},{40,32},{48,56},{56,48},{64,72... | collective-permute-start | bytes 184328 | tf_op jit(solution)/shard_map/ppermute | solution.py:19
  262.2 12.2 %collective-permute-start.11 = (f32[120,128]{1,0:T(8,128)S(1)}, f32[120,128]{1,0:T(8,128)S(1)}, u32[]{:S(2)}, u32[]{:S(2)}) collective-permute-start(f32[120,128]{1,0:T(8,128)S(1)} %slice_add_fusion), channel_id=1, source_target_pairs={{0,16},{8,24},{16,0},{24,8},{32,48},{40,56},{48,32},{56,40},{64,80... | collective-permute-start | bytes 184328 | tf_op jit(solution)/shard_map/ppermute | solution.py:19
  268.1 13.4 %collective-permute-start.7 = (bf16[512,128]{1,0:T(8,128)(2,1)S(1)}, bf16[512,128]{1,0:T(8,128)(2,1)S(1)}, u32[]{:S(2)}, u32[]{:S(2)}) collective-permute-start(bf16[512,128]{1,0:T(8,128)(2,1)S(1)} %slice.57), channel_id=1, source_target_pairs={{0,1},{1,0},{2,3},{3,2},{4,5},{5,4},{6,7},{7,6},{8,9},{9,8},{10,11... | collective-permute-start | bytes 393224 | tf_op jit(solution)/shard_map/ppermute | solution.py:19
  274.4 6.1 %collective-permute-start.12 = (f32[120,128]{1,0:T(8,128)S(1)}, f32[120,128]{1,0:T(8,128)S(1)}, u32[]{:S(2)}, u32[]{:S(2)}) collective-permute-start(f32[120,128]{1,0:T(8,128)S(1)} %add.167), channel_id=1, source_target_pairs={{0,32},{8,40},{16,48},{24,56},{32,0},{40,8},{48,16},{56,24},{64,96... | collective-permute-start | bytes 184328 | tf_op jit(solution)/shard_map/ppermute | solution.py:19
  280.4 4.3 %collective-permute-start.13 = (f32[120,128]{1,0:T(8,128)S(1)}, f32[120,128]{1,0:T(8,128)S(1)}, u32[]{:S(2)}, u32[]{:S(2)}) collective-permute-start(f32[120,128]{1,0:T(8,128)S(1)} %add.168), channel_id=1, source_target_pairs={{0,64},{8,72},{16,80},{24,88},{32,96},{40,104},{48,112},{56,120},{... | collective-permute-start | bytes 184328 | tf_op jit(solution)/shard_map/ppermute | solution.py:19
  281.5 26.7 %collective-permute-start.8 = (bf16[2,512,128]{2,1,0:T(8,128)(2,1)S(1)}, bf16[2,512,128]{2,1,0:T(8,128)(2,1)S(1)}, u32[]{:S(2)}, u32[]{:S(2)}) collective-permute-start(bf16[2,512,128]{2,1,0:T(8,128)(2,1)S(1)} %maximum_select_fusion.5), channel_id=1, source_target_pairs={{0,4},{1,5},{2,6},{3,7},{4,0},{5,1},{6,2},{7,3},{8,12},{9,13},{10,... | collective-permute-start | bytes 786440 | tf_op jit(solution)/shard_map/ppermute | solution.py:19
  284.8 5.9 %collective-permute-start.14 = (f32[120,128]{1,0:T(8,128)S(1)}, f32[120,128]{1,0:T(8,128)S(1)}, u32[]{:S(2)}, u32[]{:S(2)}) collective-permute-start(f32[120,128]{1,0:T(8,128)S(1)} %add.169), channel_id=1, source_target_pairs={{0,128},{8,136},{16,144},{24,152},{32,160},{40,168},{48,176},{56,1... | collective-permute-start | bytes 184328 | tf_op jit(solution)/shard_map/ppermute | solution.py:19
  290.6 8.4 %collective-permute-start.15 = (f32[120,128]{1,0:T(8,128)S(1)}, f32[120,128]{1,0:T(8,128)S(1)}, u32[]{:S(2)}, u32[]{:S(2)}) collective-permute-start(f32[120,128]{1,0:T(8,128)S(1)} %add.170), channel_id=1, source_target_pairs={{0,1},{1,0},{2,3},{3,2},{4,5},{5,4},{6,7},{7,6},{8,9},{9,8},{10,11... | collective-permute-start | bytes 184328 | tf_op jit(solution)/shard_map/ppermute | solution.py:19
  299.1 7.8 %collective-permute-start.16 = (f32[2,120,128]{2,1,0:T(8,128)S(1)}, f32[2,120,128]{2,1,0:T(8,128)S(1)}, u32[]{:S(2)}, u32[]{:S(2)}) collective-permute-start(f32[2,120,128]{2,1,0:T(8,128)S(1)} %maximum_select_fusion.8), channel_id=1, source_target_pairs={{0,4},{1,5},{2,6},{3,7},{4,0},{5,1},{6,2},{7,3},{8,12},{9,13},{10,... | collective-permute-start | bytes 368648 | tf_op jit(solution)/shard_map/ppermute | solution.py:19
  306.9 8.5 %collective-permute-start.17 = (f32[2,2,120,128]{3,2,1,0:T(8,128)S(1)}, f32[2,2,120,128]{3,2,1,0:T(8,128)S(1)}, u32[]{:S(2)}, u32[]{:S(2)}) collective-permute-start(f32[2,2,120,128]{3,2,1,0:T(8,128)S(1)} %maximum_select_fusion.6), channel_id=1, source_target_pairs={{0,2},{1,3},{2,0},{3,1},{4,6},{5,7},{6,4},{7,5},{8,10},{9,11},{10,... | collective-permute-start | bytes 737288 | tf_op jit(solution)/shard_map/ppermute | solution.py:19
  308.4 12.6 %collective-permute-start.9 = (bf16[2,2,512,128]{3,2,1,0:T(8,128)(2,1)S(1)}, bf16[2,2,512,128]{3,2,1,0:T(8,128)(2,1)S(1)}, u32[]{:S(2)}, u32[]{:S(2)}) collective-permute-start(bf16[2,2,512,128]{3,2,1,0:T(8,128)(2,1)S(1)} %maximum_select_fusion.2), channel_id=1, source_target_pairs={{0,2},{1,3},{2,0},{3,1},{4,6},{5,7},{6,4},{7,5},{8,10},{9,11},{10,... | collective-permute-start | bytes 1572872 | tf_op jit(solution)/shard_map/ppermute | solution.py:19

commit v3 on v2

--- a/solution.py
+++ b/solution.py
@@ -2,6 +2,7 @@
 import jax.numpy as jnp
 from jax import lax
 from jax.sharding import PartitionSpec as P
+
 
 DEGREE = 16
 
@@ -59,7 +60,7 @@
     return jnp.einsum("ef,eg->fg", a, b, preferred_element_type=jnp.float32)
 
 
-def shards(
+def layer(
     node_feats,
     saved_agg,
     node_cot,
@@ -86,8 +87,8 @@
     member = lax.axis_index("edge")
     share = nodes // groups
     start = member * share
-    upper_rows = jnp.take(node_feats, send_upper, axis=0)
-    lower_rows = jnp.take(node_feats, send_lower, axis=0)
+    upper_rows = node_feats.at[send_upper].get(mode="promise_in_bounds", unique_indices=True)
+    lower_rows = node_feats.at[send_lower].get(mode="promise_in_bounds", unique_indices=True)
     from_lower = passed_along(upper_rows, "sky", 1)
     from_upper = passed_along(lower_rows, "sky", -1)
     all_rows = jnp.concatenate([node_feats, from_lower, from_upper], axis=0)
@@ -100,7 +101,7 @@
     d_pre_node = (matmul(own_cot, v_out.T) * slope(pre_node)).astype(jnp.bfloat16)
     d_agg = matmul(d_pre_node, v_agg.T).astype(jnp.bfloat16)
     d_node = own_cot.astype(jnp.float32) + matmul(d_pre_node, v_self.T)
-    sender_rows = jnp.take(all_rows, senders, axis=0)
+    sender_rows = all_rows.at[senders].get(mode="promise_in_bounds")
     pre_edge = (
         jnp.repeat(matmul(own, w_recv), DEGREE, axis=0)
         + matmul(sender_rows, w_send)
@@ -120,13 +121,15 @@
     d_pre = (matmul(d_msg, w_out.T) * slope(pre_edge)).astype(jnp.bfloat16)
     edge_grad = matmul(d_pre, w_edge.T).astype(jnp.bfloat16)
     to_recv = matmul(d_pre, w_recv.T).reshape(share, DEGREE, width).sum(axis=1)
-    to_send = jax.ops.segment_sum(matmul(d_pre, w_send.T), senders, num_segments=nodes + 2 * halo)
+    to_send = jax.ops.segment_sum(matmul(d_pre, w_send.T), senders, num_segments=nodes + 2 * halo, mode="promise_in_bounds"
+    )
     local = to_send[:nodes]
     cot_lower = to_send[nodes : nodes + halo]
     cot_upper = to_send[nodes + halo :]
     back_upper = passed_along(cot_lower.astype(jnp.bfloat16), "sky", -1).astype(cot_lower.dtype)
     back_lower = passed_along(cot_upper.astype(jnp.bfloat16), "sky", 1).astype(cot_upper.dtype)
-    local = local.at[send_upper].add(back_upper).at[send_lower].add(back_lower)
+    local = local.at[send_upper].add(back_upper, mode="promise_in_bounds", unique_indices=True)
+    local = local.at[send_lower].add(back_lower, mode="promise_in_bounds", unique_indices=True)
     recv_grad = jnp.einsum(
         "nf,nkg->fg", own, d_pre.reshape(share, DEGREE, width), preferred_element_type=jnp.float32
     )
@@ -149,20 +152,16 @@
         ],
         axis=0,
     )
-    used = terms.shape[0]
-    chunk = -(-used // (groups * 8)) * 8
-    terms = jnp.pad(terms, ((0, chunk * groups - used), (0, 0)))
+    rounds = [("sky", bit) for bit in range(lax.axis_size("sky").bit_length() - 1)]
+    rounds += [("edge", bit) for bit in EDGE_ORDER]
+    for axis, bit in rounds:
+        got = exchanged(terms, axis, bit)
+        terms = terms + got
     mine = lax.dynamic_slice_in_dim(local, start, share, 0) + d_node + to_recv
     local = lax.dynamic_update_slice_in_dim(local, mine, start, 0)
-    packed = jnp.concatenate(
-        [local.reshape(groups, share, width), terms.reshape(groups, chunk, width)], axis=1
-    )
-    summed = halving_sum(packed, "edge", member, EDGE_ORDER)
-    node_grad = doubling_gather(summed[:share].astype(jnp.bfloat16), "edge", member, EDGE_ORDER)
-    totals = summed[share:]
-    for bit in range(lax.axis_size("sky").bit_length() - 1):
-        totals = totals + exchanged(totals, "sky", bit)
-    totals = doubling_gather(totals, "edge", member, EDGE_ORDER)[:used]
+    summed = halving_sum(local.reshape(groups, share, width), "edge", member, EDGE_ORDER)
+    node_grad = doubling_gather(summed.astype(jnp.bfloat16), "edge", member, EDGE_ORDER)
+    totals = terms
     scale = 1.0 / jnp.sqrt(jnp.float32(lax.axis_size("sky") * nodes * DEGREE))
     totals = totals * scale
     blocks = width
@@ -194,4 +193,4 @@
         P(),
     )
     out_specs = (P("sky", None), P(("sky", "edge"), None), P(), P(), P())
-    return jax.shard_map(shards, mesh=mesh, in_specs=in_specs, out_specs=out_specs, check_vma=False)
+    return jax.shard_map(layer, mesh=mesh, in_specs=in_specs, out_specs=out_specs, check_vma=False)

time: 325 us -> 328 us (level)
  waiting for transfers between devices: 83.5 us -> 93.8 us
  other arithmetic: 101 us -> 95.4 us
    ppermute x14, waiting for transfers between devices: 80 us -> 88.2 us  [exchanged(): return lax.ppermute(array, axis, [(i, i ^ 1 << bit) for i in range(size)])]
    select_n x4 -> x2, other arithmetic: 6.25 us -> 0.86 us  [the longest x1 0.85 us: layer(): node_feats.at[send_lower].get(mode='promise_in_bounds', unique_indices=True)]
    add x5 -> x7, other arithmetic: 0.05 us -> 4.36 us  [layer(): terms = terms + got]
  transfers between devices with their start and end apart: 18 -> 18, of which waited for: 11 -> 10; matrix products, arithmetic and copies ran while one was open for 16% -> 17% of each run, Pallas kernels for 0% -> 0%
where the time goes in v3:
time: 328 us; the launch traced here: 325 us
  other arithmetic  95.4 us (29%)
  waiting for transfers between devices  93.8 us (29%)
  local copies, waits for them, and re-layouts  63 us (19%)
  starting transfers between devices  43.1 us (13%)
  matrix products  28.5 us (9%)
    ppermute x14, waiting for transfers between devices, exchanged(): return lax.ppermute(array, axis, [(i, i ^ 1 << bit) for i in range(size)])  88.2 us
    scatter-add x1, other arithmetic, layer(): jax.ops.segment_sum(matmul(d_pre, w_send.T), senders, num_segments=nodes...  46.5 us
    ppermute x14, starting transfers between devices, exchanged(): return lax.ppermute(array, axis, [(i, i ^ 1 << bit) for i in range(size)])  40.8 us
    gather x1, local copies, waits for them, and re-layouts, layer(): sender_rows = all_rows.at[senders].get(mode='promise_in_bounds')  32.7 us
    dot_general x12, matrix products, matmul(): return jnp.dot(a, b, preferred_element_type=jnp.float32)  20.3 us
    scatter-add x1, other arithmetic, layer(): local.at[send_upper]  13.6 us
    scatter-add x1, other arithmetic, layer(): local.at[send_lower]  13.6 us
    gather x1, local copies, waits for them, and re-layouts, layer(): node_feats.at[send_lower].get(mode='promise_in_bounds', unique_indices=True)  9.16 us
  transfers between devices with their start and end apart: 18, of which 10 were waited for; matrix products, arithmetic and copies ran while one was open for 17% of the time, Pallas kernels for 0%

profile of v3, /device:TPU:16, one launch (start us, length us, event | category | flops | bytes accessed | tf_op | source)
XLA Modules:
  0.0 324.7 jit_solution(1140955062160957320)
XLA Ops:
  0.6 0.9 compare_select_fusion.1
  1.5 9.2 %gather_fusion.1 = bf16[2048,128]{1,0:T(8,128)(2,1)} fusion(bf16[4096,128]{1,0:T(8,128)(2,1)} %param.18, s32[2048]{0:T(1024)S(1)} %get-tuple-element.8), kind=kCustom, calls=%fused_computation.1 | custom fusion | bytes 1056768 | tf_op jit(solution)/shard_map/gather | solution.py:91
  10.7 8.1 %gather_fusion = bf16[2048,128]{1,0:T(8,128)(2,1)} fusion(bf16[4096,128]{1,0:T(8,128)(2,1)S(1)} %copy-done.1, s32[2048]{0:T(1024)S(1)} %get-tuple-element.10), kind=kCustom, calls=%fused_computation | custom fusion | bytes 1056768 | tf_op jit(solution)/shard_map/gather | solution.py:90
  19.5 1.1 fusion.8
  20.6 1.8 fusion.18
  22.4 1.7 convert_reduce_fusion.1
  24.0 1.8 fusion.19
  25.8 0.9 fusion.24
  26.6 0.9 fusion.10
  29.2 0.9 fusion.28
  30.1 3.5 %fusion.4 = bf16[8192,128]{1,0:T(8,128)(2,1)} fusion(bf16[8192,128]{1,0:T(8,128)(2,1)} %param.22, f32[8192]{0:T(1024)} %reshape.234, f32[512,128]{1,0:T(8,128)} %fusion.10), kind=kLoop, calls=%fused_computation.16 | loop fusion | flops 4194304 | bytes 4489216 | tf_op jit(solution)/shard_map/convert_element_type | solution.py:120
  34.2 2.6 fusion.44
  36.9 2.7 pad_maximum_fusion
  39.6 32.7 %gather_fusion.2 = bf16[8192,128]{1,0:T(8,128)(2,1)} fusion(bf16[8192,128]{1,0:T(8,128)(2,1)} %pad_maximum_fusion, s32[8192]{0:T(1024)} %fusion.32), kind=kCustom, calls=%fused_computation.2 | custom fusion | bytes 4227072 | tf_op jit(solution)/shard_map/gather | solution.py:104
  72.6 1.9 copy-done.6
  74.5 2.5 fusion.1
  77.1 1.9 fusion.7
  79.0 2.3 bitcast_reduce_fusion
  82.1 1.4 bitcast_reduce_fusion.1
  83.6 2.7 fusion.45
  86.2 46.5 %scatter_custom_fusion = f32[8192,128]{1,0:T(8,128)} fusion(s32[8192]{0:T(1024)} %param.23, f32[8192,128]{1,0:T(8,128)} %fusion.45, f32[]{:T(128)} %constant.28.clone.1), kind=kCustom, calls=%fused_computation.20 | custom fusion | flops 1048576 | bytes 4194816 | tf_op jit(solution)/shard_map/scatter-add | solution.py:124
  132.7 2.5 convert.6
  135.3 0.9 copy-done.7
  136.2 1.5 slice.32
  137.6 0.9 fusion.43
  138.5 1.0 collective-permute-start.3
  140.5 0.8 convolution_bitcast_fusion
  141.3 5.6 %collective-permute-done.2 = bf16[2048,128]{1,0:T(8,128)(2,1)} collective-permute-done((bf16[2048,128]{1,0:T(8,128)(2,1)S(1)}, bf16[2048,128]{1,0:T(8,128)(2,1)}, u32[]{:S(2)}, u32[]{:S(2)}) %collective-permute-start.2) | collective-permute-done | bytes 524320 | tf_op jit(solution)/shard_map/ppermute | solution.py:12
  147.0 13.6 %scatter_custom_fusion.1 = f32[4096,128]{1,0:T(8,128)} fusion(f32[4096,128]{1,0:T(8,128)} %slice.32, s32[2048]{0:T(1024)S(1)} %get-tuple-element.9, bf16[2048,128]{1,0:T(8,128)(2,1)} %collective-permute-done.2), kind=kCustom, calls=%fused_computation.37 | custom fusion | flops 524288 | bytes 2621440 | tf_op jit(solution)/shard_map/scatter-add | solution.py:131
  160.6 13.6 %scatter_custom_fusion.2 = f32[4096,128]{1,0:T(8,128)} fusion(f32[4096,128]{1,0:T(8,128)} %scatter_custom_fusion.1, s32[2048]{0:T(1024)S(1)} %get-tuple-element.7, bf16[2048,128]{1,0:T(8,128)(2,1)} %collective-permute-done.3), kind=kCustom, calls=%fused_computation.35 | custom fusion | flops 524288 | bytes 2621440 | tf_op jit(solution)/shard_map/scatter-add | solution.py:132
  174.2 2.0 add_dynamic-update-slice_fusion
  176.3 2.3 dynamic-slice_bitcast_fusion
  178.6 1.5 collective-permute-start.4
  180.1 1.1 convert_reduce_fusion
  181.3 2.9 collective-permute-start.10
  184.2 1.4 collective-permute-done.10
  185.7 3.8 %collective-permute-start.11 = (f32[898,128]{1,0:T(8,128)S(1)}, f32[898,128]{1,0:T(8,128)S(1)}, u32[]{:S(2)}, u32[]{:S(2)}) collective-permute-start(f32[898,128]{1,0:T(8,128)S(1)} %add.167), channel_id=1, source_target_pairs={{0,16},{8,24},{16,0},{24,8},{32,48},{40,56},{48,32},{56,40},{64,80... | collective-permute-start | bytes 1379336 | tf_op jit(solution)/shard_map/ppermute | solution.py:20
  189.5 11.1 %collective-permute-done.11 = f32[898,128]{1,0:T(8,128)S(1)} collective-permute-done((f32[898,128]{1,0:T(8,128)S(1)}, f32[898,128]{1,0:T(8,128)S(1)}, u32[]{:S(2)}, u32[]{:S(2)}) %collective-permute-start.11) | collective-permute-done | bytes 459808 | tf_op jit(solution)/shard_map/ppermute | solution.py:20
  200.7 5.7 %collective-permute-start.12 = (f32[898,128]{1,0:T(8,128)S(1)}, f32[898,128]{1,0:T(8,128)S(1)}, u32[]{:S(2)}, u32[]{:S(2)}) collective-permute-start(f32[898,128]{1,0:T(8,128)S(1)} %add.168), channel_id=1, source_target_pairs={{0,32},{8,40},{16,48},{24,56},{32,0},{40,8},{48,16},{56,24},{64,96... | collective-permute-start | bytes 1379336 | tf_op jit(solution)/shard_map/ppermute | solution.py:20
  206.4 1.6 bitcast_add_fusion.1
  208.0 0.8 dynamic-slice_bitcast_fusion.1
  208.9 2.7 collective-permute-start.5
  211.6 5.0 %collective-permute-done.12 = f32[898,128]{1,0:T(8,128)S(1)} collective-permute-done((f32[898,128]{1,0:T(8,128)S(1)}, f32[898,128]{1,0:T(8,128)S(1)}, u32[]{:S(2)}, u32[]{:S(2)}) %collective-permute-start.12) | collective-permute-done | bytes 459808 | tf_op jit(solution)/shard_map/ppermute | solution.py:20
  216.6 0.8 add.169
  217.5 11.6 %collective-permute-done.13 = f32[898,128]{1,0:T(8,128)} collective-permute-done((f32[898,128]{1,0:T(8,128)}, f32[898,128]{1,0:T(8,128)}, u32[]{:S(2)}, u32[]{:S(2)}) %collective-permute-start.13) | collective-permute-done | bytes 459808 | tf_op jit(solution)/shard_map/ppermute | solution.py:20
  229.1 1.2 add.170
  230.3 5.6 %collective-permute-start.14 = (f32[898,128]{1,0:T(8,128)S(1)}, f32[898,128]{1,0:T(8,128)S(1)}, u32[]{:S(2)}, u32[]{:S(2)}) collective-permute-start(f32[898,128]{1,0:T(8,128)S(1)} %add.170), channel_id=1, source_target_pairs={{0,128},{8,136},{16,144},{24,152},{32,160},{40,168},{48,176},{56,1... | collective-permute-start | bytes 1379336 | tf_op jit(solution)/shard_map/ppermute | solution.py:20
  235.9 1.1 bitcast_add_fusion.2
  237.0 0.8 copy-done.10
  237.8 4.6 %collective-permute-start.6 = (f32[512,128]{1,0:T(8,128)S(1)}, f32[512,128]{1,0:T(8,128)S(1)}, u32[]{:S(2)}, u32[]{:S(2)}) collective-permute-start(f32[512,128]{1,0:T(8,128)S(1)} %dynamic-slice_bitcast_fusion.2), channel_id=1, source_target_pairs={{0,1},{1,0},{2,3},{3,2},{4,5},{5,4},{6,7},{7,6},{8,9},{9,8},{10,11... | collective-permute-start | bytes 786440 | tf_op jit(solution)/shard_map/ppermute | solution.py:20
  242.4 23.9 %collective-permute-done.14 = f32[898,128]{1,0:T(8,128)S(1)} collective-permute-done((f32[898,128]{1,0:T(8,128)S(1)}, f32[898,128]{1,0:T(8,128)S(1)}, u32[]{:S(2)}, u32[]{:S(2)}) %collective-permute-start.14) | collective-permute-done | bytes 459808 | tf_op jit(solution)/shard_map/ppermute | solution.py:20
  267.0 1.0 fusion.16
  268.0 4.6 %collective-permute-start.7 = (bf16[512,128]{1,0:T(8,128)(2,1)S(1)}, bf16[512,128]{1,0:T(8,128)(2,1)S(1)}, u32[]{:S(2)}, u32[]{:S(2)}) collective-permute-start(bf16[512,128]{1,0:T(8,128)(2,1)S(1)} %fusion.16), channel_id=1, source_target_pairs={{0,1},{1,0},{2,3},{3,2},{4,5},{5,4},{6,7},{7,6},{8,9},{9,8},{10,11... | collective-permute-start | bytes 393224 | tf_op jit(solution)/shard_map/ppermute | solution.py:20
  272.5 5.6 %collective-permute-done.15 = f32[898,128]{1,0:T(8,128)} collective-permute-done((f32[898,128]{1,0:T(8,128)S(1)}, f32[898,128]{1,0:T(8,128)}, u32[]{:S(2)}, u32[]{:S(2)}) %collective-permute-start.15) | collective-permute-done | bytes 459808 | tf_op jit(solution)/shard_map/ppermute | solution.py:20
  278.2 1.1 add.172
  279.3 2.8 collective-permute-start.16
  282.8 0.8 collective-permute-start.8
  283.7 13.6 %collective-permute-done.8 = bf16[2,512,128]{2,1,0:T(8,128)(2,1)S(1)} collective-permute-done((bf16[2,512,128]{2,1,0:T(8,128)(2,1)}, bf16[2,512,128]{2,1,0:T(8,128)(2,1)S(1)}, u32[]{:S(2)}, u32[]{:S(2)}) %collective-permute-start.8) | collective-permute-done | bytes 262176 | tf_op jit(solution)/shard_map/ppermute | solution.py:20
  298.0 1.1 add.173
  299.0 4.6 %collective-permute-start.17 = (f32[898,128]{1,0:T(8,128)S(1)}, f32[898,128]{1,0:T(8,128)S(1)}, u32[]{:S(2)}, u32[]{:S(2)}) collective-permute-start(f32[898,128]{1,0:T(8,128)S(1)} %add.173), channel_id=1, source_target_pairs={{0,1},{1,0},{2,3},{3,2},{4,5},{5,4},{6,7},{7,6},{8,9},{9,8},{10,11... | collective-permute-start | bytes 1379336 | tf_op jit(solution)/shard_map/ppermute | solution.py:20
  303.6 2.0 convolution_convert_fusion
  305.8 2.9 collective-permute-done.9
  308.7 1.1 maximum_select_fusion
  309.8 12.9 %collective-permute-done.17 = f32[898,128]{1,0:T(8,128)S(1)} collective-permute-done((f32[898,128]{1,0:T(8,128)S(1)}, f32[898,128]{1,0:T(8,128)S(1)}, u32[]{:S(2)}, u32[]{:S(2)}) %collective-permute-start.17) | collective-permute-done | bytes 459808 | tf_op jit(solution)/shard_map/ppermute | solution.py:20
  (94 shorter events, 9.6 us)
Async XLA Ops:
  0.6 33.6 %copy-start = (bf16[8192,128]{1,0:T(8,128)(2,1)S(1)}, bf16[8192,128]{1,0:T(8,128)(2,1)}, u32[]{:S(2)}) copy-start(bf16[8192,128]{1,0:T(8,128)(2,1)} %param.21) | copy-start | bytes 6291460
  1.5 9.2 %copy-start.24 = (s32[2048]{0:T(1024)S(1)}, s32[2048]{0:T(1024)}, u32[]{:S(2)}) copy-start(s32[2048]{0:T(1024)} %param.26) | copy-start | bytes 24580
  1.5 9.2 %copy-start.1 = (bf16[4096,128]{1,0:T(8,128)(2,1)S(1)}, bf16[4096,128]{1,0:T(8,128)(2,1)}, u32[]{:S(2)}) copy-start(bf16[4096,128]{1,0:T(8,128)(2,1)} %param.18) | copy-start | bytes 3145732
  10.7 26.2 %collective-permute-start.1 = (bf16[2048,128]{1,0:T(8,128)(2,1)}, bf16[2048,128]{1,0:T(8,128)(2,1)}, u32[]{:S(2)}, u32[]{:S(2)}) collective-permute-start(bf16[2048,128]{1,0:T(8,128)(2,1)} %gather_fusion.1), channel_id=1, source_target_pairs={{0,248},{8,0},{16,8},{24,16},{32,24},{40,32},{48,40},{56,48},{64,5... | collective-permute-start | bytes 1572872 | tf_op jit(solution)/shard_map/ppermute | solution.py:12
  10.7 8.6 %copy-start.17 = (bf16[128,128]{1,0:T(8,128)(2,1)S(1)}, bf16[128,128]{1,0:T(8,128)(2,1)}, u32[]{:S(2)}) copy-start(bf16[128,128]{1,0:T(8,128)(2,1)} %param.32) | copy-start | bytes 98308
  10.7 8.8 %copy-start.19 = (bf16[128,128]{1,0:T(8,128)(2,1)S(1)}, bf16[128,128]{1,0:T(8,128)(2,1)}, u32[]{:S(2)}) copy-start(bf16[128,128]{1,0:T(8,128)(2,1)} %param.33) | copy-start | bytes 98308
  10.7 8.8 %copy-start.27 = (f32[128]{0:T(128)S(1)}, f32[128]{0:T(128)}, u32[]{:S(2)}) copy-start(f32[128]{0:T(128)} %param.35) | copy-start | bytes 1540
  18.8 3.6 %copy-start.28 = (bf16[128,128]{1,0:T(8,128)(2,1)S(1)}, bf16[128,128]{1,0:T(8,128)(2,1)}, u32[]{:S(2)}) copy-start(bf16[128,128]{1,0:T(8,128)(2,1)} %param.34) | copy-start | bytes 98308
  18.8 18.1 %collective-permute-start = (bf16[2048,128]{1,0:T(8,128)(2,1)}, bf16[2048,128]{1,0:T(8,128)(2,1)}, u32[]{:S(2)}, u32[]{:S(2)}) collective-permute-start(bf16[2048,128]{1,0:T(8,128)(2,1)} %gather_fusion), channel_id=1, source_target_pairs={{0,8},{8,16},{16,24},{24,32},{32,40},{40,48},{48,56},{56,64},{64,7... | collective-permute-start | bytes 1572872 | tf_op jit(solution)/shard_map/ppermute | solution.py:12
  30.1 3.5 %copy-start.22 = (s32[8192]{0:T(1024)S(1)}, s32[8192]{0:T(1024)}, u32[]{:S(2)}) copy-start(s32[8192]{0:T(1024)} %param.23) | copy-start | bytes 98308
  30.1 4.1 %copy-start.15 = (bf16[128,128]{1,0:T(8,128)(2,1)S(1)}, bf16[128,128]{1,0:T(8,128)(2,1)}, u32[]{:S(2)}) copy-start(bf16[128,128]{1,0:T(8,128)(2,1)} %param.29) | copy-start | bytes 98308
  72.3 2.2 copy-start.6
  72.3 2.2 copy-start.14
  72.3 2.2 copy-start.25
  74.5 2.6 copy-start.9
  77.1 2.0 copy-start.29
  79.0 2.3 copy-start.8
  81.3 2.3 copy-start.2
  81.3 0.8 copy-start.23
  132.7 3.4 %copy-start.7 = (f32[8192,128]{1,0:T(8,128)S(1)}, f32[8192,128]{1,0:T(8,128)}, u32[]{:S(2)}) copy-start(f32[8192,128]{1,0:T(8,128)} %scatter_custom_fusion) | copy-start | bytes 12582916
  137.6 2.8 copy-start.3
  138.5 22.1 %collective-permute-start.3 = (bf16[2048,128]{1,0:T(8,128)(2,1)}, bf16[2048,128]{1,0:T(8,128)(2,1)}, u32[]{:S(2)}, u32[]{:S(2)}) collective-permute-start(bf16[2048,128]{1,0:T(8,128)(2,1)} %get-tuple-element.5), channel_id=1, source_target_pairs={{0,8},{8,16},{16,24},{24,32},{32,40},{40,48},{48,56},{56,64},{64,7... | collective-permute-start | bytes 1572872 | tf_op jit(solution)/shard_map/ppermute | solution.py:12
  139.6 7.4 %collective-permute-start.2 = (bf16[2048,128]{1,0:T(8,128)(2,1)S(1)}, bf16[2048,128]{1,0:T(8,128)(2,1)}, u32[]{:S(2)}, u32[]{:S(2)}) collective-permute-start(bf16[2048,128]{1,0:T(8,128)(2,1)S(1)} %get-tuple-element.6), channel_id=1, source_target_pairs={{0,248},{8,0},{16,8},{24,16},{32,24},{40,32},{48,40},{56,48},{64,5... | collective-permute-start | bytes 1572872 | tf_op jit(solution)/shard_map/ppermute | solution.py:12
  147.0 27.3 %copy-start.13 = (f32[512,128]{1,0:T(8,128)S(1)}, f32[512,128]{1,0:T(8,128)}, u32[]{:S(2)}) copy-start(f32[512,128]{1,0:T(8,128)} %bitcast_reduce_fusion.1) | copy-start | bytes 786436
  147.0 27.3 %copy-start.18 = (bf16[128,128]{1,0:T(8,128)(2,1)S(1)}, bf16[128,128]{1,0:T(8,128)(2,1)}, u32[]{:S(2)}) copy-start(bf16[128,128]{1,0:T(8,128)(2,1)} %param.32) | copy-start | bytes 98308
  174.2 5.8 %copy-start.4 = (bf16[8192,128]{1,0:T(8,128)(2,1)S(1)}, bf16[8192,128]{1,0:T(8,128)(2,1)}, u32[]{:S(2)}) copy-start(bf16[8192,128]{1,0:T(8,128)(2,1)} %copy-done.2) | copy-start | bytes 6291460
  176.2 4.9 %copy-start.11 = (f32[128,128]{1,0:T(8,128)S(1)}, f32[128,128]{1,0:T(8,128)}, u32[]{:S(2)}) copy-start(f32[128,128]{1,0:T(8,128)} %fusion.19) | copy-start | bytes 196612
  176.2 4.9 %copy-start.12 = (f32[128,128]{1,0:T(8,128)S(1)}, f32[128,128]{1,0:T(8,128)}, u32[]{:S(2)}) copy-start(f32[128,128]{1,0:T(8,128)} %fusion.24) | copy-start | bytes 196612
  176.2 4.9 %copy-start.20 = (f32[128,128]{1,0:T(8,128)S(1)}, f32[128,128]{1,0:T(8,128)}, u32[]{:S(2)}) copy-start(f32[128,128]{1,0:T(8,128)} %fusion.18) | copy-start | bytes 196612
  176.3 4.9 %copy-start.21 = (f32[128,128]{1,0:T(8,128)S(1)}, f32[128,128]{1,0:T(8,128)}, u32[]{:S(2)}) copy-start(f32[128,128]{1,0:T(8,128)} %fusion.7) | copy-start | bytes 196612
  176.3 4.9 %copy-start.26 = (f32[128]{0:T(128)S(1)}, f32[128]{0:T(128)}, u32[]{:S(2)}) copy-start(f32[128]{0:T(128)} %get-tuple-element.13) | copy-start | bytes 1540
  178.6 27.8 %collective-permute-start.4 = (f32[2,2,512,128]{3,2,1,0:T(8,128)}, f32[2,2,512,128]{3,2,1,0:T(8,128)}, u32[]{:S(2)}, u32[]{:S(2)}) collective-permute-start(f32[2,2,512,128]{3,2,1,0:T(8,128)} %dynamic-slice_bitcast_fusion), channel_id=1, source_target_pairs={{0,2},{1,3},{2,0},{3,1},{4,6},{5,7},{6,4},{7,5},{8,10},{9,11},{10,... | collective-permute-start | bytes 3145736 | tf_op jit(solution)/shard_map/ppermute | solution.py:20
  181.3 4.4 %collective-permute-start.10 = (f32[898,128]{1,0:T(8,128)S(1)}, f32[898,128]{1,0:T(8,128)S(1)}, u32[]{:S(2)}, u32[]{:S(2)}) collective-permute-start(f32[898,128]{1,0:T(8,128)S(1)} %concatenate.53), channel_id=1, source_target_pairs={{0,8},{8,0},{16,24},{24,16},{32,40},{40,32},{48,56},{56,48},{64,72... | collective-permute-start | bytes 1379336 | tf_op jit(solution)/shard_map/ppermute | solution.py:20
  185.7 15.0 %collective-permute-start.11 = (f32[898,128]{1,0:T(8,128)S(1)}, f32[898,128]{1,0:T(8,128)S(1)}, u32[]{:S(2)}, u32[]{:S(2)}) collective-permute-start(f32[898,128]{1,0:T(8,128)S(1)} %add.167), channel_id=1, source_target_pairs={{0,16},{8,24},{16,0},{24,8},{32,48},{40,56},{48,32},{56,40},{64,80... | collective-permute-start | bytes 1379336 | tf_op jit(solution)/shard_map/ppermute | solution.py:20
  200.7 15.8 %collective-permute-start.12 = (f32[898,128]{1,0:T(8,128)S(1)}, f32[898,128]{1,0:T(8,128)S(1)}, u32[]{:S(2)}, u32[]{:S(2)}) collective-permute-start(f32[898,128]{1,0:T(8,128)S(1)} %add.168), channel_id=1, source_target_pairs={{0,32},{8,40},{16,48},{24,56},{32,0},{40,8},{48,16},{56,24},{64,96... | collective-permute-start | bytes 1379336 | tf_op jit(solution)/shard_map/ppermute | solution.py:20
  208.9 27.0 %collective-permute-start.5 = (f32[2,512,128]{2,1,0:T(8,128)}, f32[2,512,128]{2,1,0:T(8,128)}, u32[]{:S(2)}, u32[]{:S(2)}) collective-permute-start(f32[2,512,128]{2,1,0:T(8,128)} %dynamic-slice_bitcast_fusion.1), channel_id=1, source_target_pairs={{0,4},{1,5},{2,6},{3,7},{4,0},{5,1},{6,2},{7,3},{8,12},{9,13},{10,... | collective-permute-start | bytes 1572872 | tf_op jit(solution)/shard_map/ppermute | solution.py:20
  217.4 11.7 %collective-permute-start.13 = (f32[898,128]{1,0:T(8,128)}, f32[898,128]{1,0:T(8,128)}, u32[]{:S(2)}, u32[]{:S(2)}) collective-permute-start(f32[898,128]{1,0:T(8,128)} %add.169), channel_id=1, source_target_pairs={{0,64},{8,72},{16,80},{24,88},{32,96},{40,104},{48,112},{56,120},{... | collective-permute-start | bytes 1379336 | tf_op jit(solution)/shard_map/ppermute | solution.py:20
  230.3 36.0 %collective-permute-start.14 = (f32[898,128]{1,0:T(8,128)S(1)}, f32[898,128]{1,0:T(8,128)S(1)}, u32[]{:S(2)}, u32[]{:S(2)}) collective-permute-start(f32[898,128]{1,0:T(8,128)S(1)} %add.170), channel_id=1, source_target_pairs={{0,128},{8,136},{16,144},{24,152},{32,160},{40,168},{48,176},{56,1... | collective-permute-start | bytes 1379336 | tf_op jit(solution)/shard_map/ppermute | solution.py:20
  237.0 0.8 copy-start.10
  237.8 29.2 %collective-permute-start.6 = (f32[512,128]{1,0:T(8,128)S(1)}, f32[512,128]{1,0:T(8,128)S(1)}, u32[]{:S(2)}, u32[]{:S(2)}) collective-permute-start(f32[512,128]{1,0:T(8,128)S(1)} %dynamic-slice_bitcast_fusion.2), channel_id=1, source_target_pairs={{0,1},{1,0},{2,3},{3,2},{4,5},{5,4},{6,7},{7,6},{8,9},{9,8},{10,11... | collective-permute-start | bytes 786440 | tf_op jit(solution)/shard_map/ppermute | solution.py:20
  266.4 11.8 %collective-permute-start.15 = (f32[898,128]{1,0:T(8,128)S(1)}, f32[898,128]{1,0:T(8,128)}, u32[]{:S(2)}, u32[]{:S(2)}) collective-permute-start(f32[898,128]{1,0:T(8,128)S(1)} %add.171), channel_id=1, source_target_pairs={{0,2},{1,3},{2,0},{3,1},{4,6},{5,7},{6,4},{7,5},{8,10},{9,11},{10,... | collective-permute-start | bytes 1379336 | tf_op jit(solution)/shard_map/ppermute | solution.py:20
  268.0 14.1 %collective-permute-start.7 = (bf16[512,128]{1,0:T(8,128)(2,1)S(1)}, bf16[512,128]{1,0:T(8,128)(2,1)S(1)}, u32[]{:S(2)}, u32[]{:S(2)}) collective-permute-start(bf16[512,128]{1,0:T(8,128)(2,1)S(1)} %fusion.16), channel_id=1, source_target_pairs={{0,1},{1,0},{2,3},{3,2},{4,5},{5,4},{6,7},{7,6},{8,9},{9,8},{10,11... | collective-permute-start | bytes 393224 | tf_op jit(solution)/shard_map/ppermute | solution.py:20
  279.3 24.3 %copy-start.16 = (bf16[128,128]{1,0:T(8,128)(2,1)S(1)}, bf16[128,128]{1,0:T(8,128)(2,1)}, u32[]{:S(2)}) copy-start(bf16[128,128]{1,0:T(8,128)(2,1)} %param.29) | copy-start | bytes 98308
  279.3 18.7 %collective-permute-start.16 = (f32[898,128]{1,0:T(8,128)S(1)}, f32[898,128]{1,0:T(8,128)}, u32[]{:S(2)}, u32[]{:S(2)}) collective-permute-start(f32[898,128]{1,0:T(8,128)S(1)} %add.172), channel_id=1, source_target_pairs={{0,4},{1,5},{2,6},{3,7},{4,0},{5,1},{6,2},{7,3},{8,12},{9,13},{10,... | collective-permute-start | bytes 1379336 | tf_op jit(solution)/shard_map/ppermute | solution.py:20
  282.8 14.5 %collective-permute-start.8 = (bf16[2,512,128]{2,1,0:T(8,128)(2,1)}, bf16[2,512,128]{2,1,0:T(8,128)(2,1)S(1)}, u32[]{:S(2)}, u32[]{:S(2)}) collective-permute-start(bf16[2,512,128]{2,1,0:T(8,128)(2,1)} %maximum_select_fusion.3), channel_id=1, source_target_pairs={{0,4},{1,5},{2,6},{3,7},{4,0},{5,1},{6,2},{7,3},{8,12},{9,13},{10,... | collective-permute-start | bytes 786440 | tf_op jit(solution)/shard_map/ppermute | solution.py:20
  283.6 20.0 %copy-start.5 = (bf16[8192,128]{1,0:T(8,128)(2,1)S(1)}, bf16[8192,128]{1,0:T(8,128)(2,1)}, u32[]{:S(2)}) copy-start(bf16[8192,128]{1,0:T(8,128)(2,1)} %copy-done.2) | copy-start | bytes 6291460
  297.3 11.3 %collective-permute-start.9 = (bf16[2,2,512,128]{3,2,1,0:T(8,128)(2,1)S(1)}, bf16[2,2,512,128]{3,2,1,0:T(8,128)(2,1)S(1)}, u32[]{:S(2)}, u32[]{:S(2)}) collective-permute-start(bf16[2,2,512,128]{3,2,1,0:T(8,128)(2,1)S(1)} %maximum_select_fusion.1), channel_id=1, source_target_pairs={{0,2},{1,3},{2,0},{3,1},{4,6},{5,7},{6,4},{7,5},{8,10},{9,11},{10,... | collective-permute-start | bytes 1572872 | tf_op jit(solution)/shard_map/ppermute | solution.py:20
  299.0 23.6 %collective-permute-start.17 = (f32[898,128]{1,0:T(8,128)S(1)}, f32[898,128]{1,0:T(8,128)S(1)}, u32[]{:S(2)}, u32[]{:S(2)}) collective-permute-start(f32[898,128]{1,0:T(8,128)S(1)} %add.173), channel_id=1, source_target_pairs={{0,1},{1,0},{2,3},{3,2},{4,5},{5,4},{6,7},{7,6},{8,9},{9,8},{10,11... | collective-permute-start | bytes 1379336 | tf_op jit(solution)/shard_map/ppermute | solution.py:20

commit v4 on v3

--- a/solution.py
+++ b/solution.py
@@ -13,6 +13,7 @@
 
 
 EDGE_ORDER = (1, 2, 0)
+EARLY_ROUNDS = 3
 
 
 def exchanged(array, axis, bit):
@@ -152,16 +153,25 @@
         ],
         axis=0,
     )
-    rounds = [("sky", bit) for bit in range(lax.axis_size("sky").bit_length() - 1)]
-    rounds += [("edge", bit) for bit in EDGE_ORDER]
-    for axis, bit in rounds:
-        got = exchanged(terms, axis, bit)
+    used = terms.shape[0]
+    chunk = -(-used // (groups * 8)) * 8
+    terms = jnp.pad(terms, ((0, chunk * groups - used), (0, 0)))
+    sky_bits = lax.axis_size("sky").bit_length() - 1
+    early = min(EARLY_ROUNDS, sky_bits)
+    for bit in range(early):
+        got = exchanged(terms, "sky", bit)
         terms = terms + got
     mine = lax.dynamic_slice_in_dim(local, start, share, 0) + d_node + to_recv
     local = lax.dynamic_update_slice_in_dim(local, mine, start, 0)
-    summed = halving_sum(local.reshape(groups, share, width), "edge", member, EDGE_ORDER)
-    node_grad = doubling_gather(summed.astype(jnp.bfloat16), "edge", member, EDGE_ORDER)
-    totals = terms
+    packed = jnp.concatenate(
+        [local.reshape(groups, share, width), terms.reshape(groups, chunk, width)], axis=1
+    )
+    summed = halving_sum(packed, "edge", member, EDGE_ORDER)
+    node_grad = doubling_gather(summed[:share].astype(jnp.bfloat16), "edge", member, EDGE_ORDER)
+    totals = summed[share:]
+    for bit in range(early, sky_bits):
+        totals = totals + exchanged(totals, "sky", bit)
+    totals = doubling_gather(totals, "edge", member, EDGE_ORDER)[:used]
     scale = 1.0 / jnp.sqrt(jnp.float32(lax.axis_size("sky") * nodes * DEGREE))
     totals = totals * scale
     blocks = width

time: 328 us -> 321 us (0.979)
  starting transfers between devices: 43.1 us -> 32.3 us
  other arithmetic: 95.4 us -> 91.5 us
    ppermute x14, starting transfers between devices: 40.8 us -> 29.5 us  [exchanged(): return lax.ppermute(array, axis, [(i, i ^ 1 << bit) for i in range(size)])]
    ppermute x14, waiting for transfers between devices: 88.2 us -> 94.7 us  [exchanged(): return lax.ppermute(array, axis, [(i, i ^ 1 << bit) for i in range(size)])]
    ppermute x4, waiting for transfers between devices: 5.65 us -> 0.01 us  [passed_along(): lax.ppermute(array, axis, [(i, (i + by) % size) for i in range(size)])]
  transfers between devices with their start and end apart: 18 -> 18, of which waited for: 10 -> 10; matrix products, arithmetic and copies ran while one was open for 17% -> 37% of each run, Pallas kernels for 0% -> 0%
where the time goes in v4:
time: 321 us; the launch traced here: 316 us
  waiting for transfers between devices  94.7 us (30%)
  other arithmetic  91.5 us (29%)
  local copies, waits for them, and re-layouts  66 us (21%)
  starting transfers between devices  32.3 us (10%)
  matrix products  29.9 us (9%)
    ppermute x14, waiting for transfers between devices, exchanged(): return lax.ppermute(array, axis, [(i, i ^ 1 << bit) for i in range(size)])  94.7 us
    scatter-add x1, other arithmetic, layer(): jax.ops.segment_sum(matmul(d_pre, w_send.T), senders, num_segments=nodes...  46.4 us
    gather x1, local copies, waits for them, and re-layouts, layer(): sender_rows = all_rows.at[senders].get(mode='promise_in_bounds')  32.7 us
    ppermute x14, starting transfers between devices, exchanged(): return lax.ppermute(array, axis, [(i, i ^ 1 << bit) for i in range(size)])  29.5 us
    dot_general x12, matrix products, matmul(): return jnp.dot(a, b, preferred_element_type=jnp.float32)  21.1 us
    scatter-add x1, other arithmetic, layer(): local.at[send_upper]  13.7 us
    scatter-add x1, other arithmetic, layer(): local.at[send_lower]  13.6 us
    gather x1, local copies, waits for them, and re-layouts, layer(): node_feats.at[send_lower].get(mode='promise_in_bounds', unique_indices=True)  9.16 us
  transfers between devices with their start and end apart: 18, of which 10 were waited for; matrix products, arithmetic and copies ran while one was open for 37% of the time, Pallas kernels for 0%

profile of v4, /device:TPU:16, one launch (start us, length us, event | category | flops | bytes accessed | tf_op | source)
XLA Modules:
  0.0 315.5 jit_solution(17857660146300038570)
XLA Ops:
  0.6 0.9 compare_select_fusion.1
  1.5 9.2 %gather_fusion.1 = bf16[2048,128]{1,0:T(8,128)(2,1)} fusion(bf16[4096,128]{1,0:T(8,128)(2,1)} %param.18, s32[2048]{0:T(1024)S(1)} %get-tuple-element.8), kind=kCustom, calls=%fused_computation.1 | custom fusion | bytes 1056768 | tf_op jit(solution)/shard_map/gather | solution.py:92
  10.7 8.1 %gather_fusion = bf16[2048,128]{1,0:T(8,128)(2,1)} fusion(bf16[4096,128]{1,0:T(8,128)(2,1)S(1)} %copy-done.1, s32[2048]{0:T(1024)S(1)} %get-tuple-element.10), kind=kCustom, calls=%fused_computation | custom fusion | bytes 1056768 | tf_op jit(solution)/shard_map/gather | solution.py:91
  19.5 1.1 fusion.13
  20.6 1.8 fusion.23
  22.4 1.7 convert_reduce_fusion.1
  24.0 1.8 fusion.24
  25.8 0.9 fusion.29
  26.6 0.9 fusion.15
  27.5 0.8 dynamic_slice.39
  28.4 0.7 reshape.421
  29.2 0.9 fusion.33
  30.1 3.5 %fusion.4 = bf16[8192,128]{1,0:T(8,128)(2,1)} fusion(bf16[8192,128]{1,0:T(8,128)(2,1)} %param.22, f32[8192]{0:T(1024)} %reshape.421, f32[512,128]{1,0:T(8,128)} %fusion.15), kind=kLoop, calls=%fused_computation.16 | loop fusion | flops 4194304 | bytes 4489216 | tf_op jit(solution)/shard_map/convert_element_type | solution.py:121
  34.2 2.6 fusion.49
  36.9 2.7 pad_maximum_fusion
  39.5 32.7 %gather_fusion.2 = bf16[8192,128]{1,0:T(8,128)(2,1)} fusion(bf16[8192,128]{1,0:T(8,128)(2,1)} %pad_maximum_fusion, s32[8192]{0:T(1024)} %fusion.37), kind=kCustom, calls=%fused_computation.2 | custom fusion | bytes 4227072 | tf_op jit(solution)/shard_map/gather | solution.py:105
  72.5 1.9 copy-done.5
  74.4 2.5 fusion.1
  77.0 1.9 fusion.7
  79.0 2.3 bitcast_reduce_fusion
  81.3 0.7 fusion.51
  82.0 1.6 convert_reduce_fusion
  83.6 0.8 convolution_bitcast_fusion
  84.4 0.9 fusion.31
  85.3 3.2 %concatenate.108 = f32[898,128]{1,0:T(8,128)S(1)} concatenate(f32[128,128]{1,0:T(8,128)} %fusion.31, f32[128,128]{1,0:T(8,128)S(1)} %fusion.51, f32[128,128]{1,0:T(8,128)S(1)} %convolution_bitcast_fusion, f32[128,128]{1,0:T(8,128)} %fusion.7, f32[128,128]{1,0:T(8,128)S(1)} %copy-done.10, f32[128,128]{1,0:T(8,128)S(1)} %copy-done.9, f32[128,128]{1,0:T(8,128)} %fusion.23, ...), dimensions={0} | concatenate | bytes 919552 | tf_op jit(solution)/shard_map/concatenate | solution.py:143
  88.6 1.3 collective-permute-start.4
  89.9 4.3 %fusion.50 = f32[8192,128]{1,0:T(8,128)} fusion(bf16[8192,128]{1,0:T(8,128)(2,1)} %copy-done.2, bf16[128,128]{1,0:T(8,128)(2,1)} %param.28), kind=kOutput, calls=%fused_computation.106 | convolution fusion | flops 268435456 | bytes 6324224 | tf_op jit(solution)/shard_map/dot_general | solution.py:57
  94.2 46.4 %scatter_custom_fusion = f32[8192,128]{1,0:T(8,128)} fusion(s32[8192]{0:T(1024)} %param.23, f32[8192,128]{1,0:T(8,128)} %fusion.50, f32[]{:T(128)} %constant.29.clone.1), kind=kCustom, calls=%fused_computation.24 | custom fusion | flops 1048576 | bytes 4194816 | tf_op jit(solution)/shard_map/scatter-add | solution.py:125
  140.7 2.4 convert.9
  143.1 1.1 pad_add_fusion
  144.2 3.5 %collective-permute-start.5 = (f32[960,128]{1,0:T(8,128)S(1)}, f32[960,128]{1,0:T(8,128)S(1)}, u32[]{:S(2)}, u32[]{:S(2)}) collective-permute-start(f32[960,128]{1,0:T(8,128)S(1)} %pad_add_fusion), channel_id=1, source_target_pairs={{0,16},{8,24},{16,0},{24,8},{32,48},{40,56},{48,32},{56,40},{64,80... | collective-permute-start | bytes 1474568 | tf_op jit(solution)/shard_map/ppermute | solution.py:21
  147.6 1.0 fusion.48
  148.7 2.3 collective-permute-start.2
  151.0 8.3 %collective-permute-done.5 = f32[960,128]{1,0:T(8,128)S(1)} collective-permute-done((f32[960,128]{1,0:T(8,128)S(1)}, f32[960,128]{1,0:T(8,128)S(1)}, u32[]{:S(2)}, u32[]{:S(2)}) %collective-permute-start.5) | collective-permute-done | bytes 491552 | tf_op jit(solution)/shard_map/ppermute | solution.py:21
  159.3 4.0 %collective-permute-start.6 = (f32[960,128]{1,0:T(8,128)S(1)}, f32[960,128]{1,0:T(8,128)S(1)}, u32[]{:S(2)}, u32[]{:S(2)}) collective-permute-start(f32[960,128]{1,0:T(8,128)S(1)} %add.152), channel_id=1, source_target_pairs={{0,32},{8,40},{16,48},{24,56},{32,0},{40,8},{48,16},{56,24},{64,96... | collective-permute-start | bytes 1474568 | tf_op jit(solution)/shard_map/ppermute | solution.py:21
  163.3 3.2 %slice.45 = f32[4096,128]{1,0:T(8,128)} slice(f32[8192,128]{1,0:T(8,128)} %scatter_custom_fusion), slice={[0:4096], [0:128]} | slice | bytes 4194304 | tf_op jit(solution)/shard_map/slice | solution.py:127
  166.6 0.7 bitcast_reduce_fusion.1
  167.3 13.7 %scatter_custom_fusion.1 = f32[4096,128]{1,0:T(8,128)} fusion(f32[4096,128]{1,0:T(8,128)} %slice.45, s32[2048]{0:T(1024)S(1)} %get-tuple-element.9, bf16[2048,128]{1,0:T(8,128)(2,1)} %collective-permute-done.2), kind=kCustom, calls=%fused_computation.45 | custom fusion | flops 524288 | bytes 2621440 | tf_op jit(solution)/shard_map/scatter-add | solution.py:132
  181.0 13.6 %scatter_custom_fusion.2 = f32[4096,128]{1,0:T(8,128)} fusion(f32[4096,128]{1,0:T(8,128)} %scatter_custom_fusion.1, s32[2048]{0:T(1024)S(1)} %get-tuple-element.7, bf16[2048,128]{1,0:T(8,128)(2,1)} %collective-permute-done.3), kind=kCustom, calls=%fused_computation.43 | custom fusion | flops 524288 | bytes 2621440 | tf_op jit(solution)/shard_map/scatter-add | solution.py:133
  194.6 1.9 add_dynamic-update-slice_fusion
  196.6 0.8 copy-done.7
  197.4 1.3 fusion.9
  198.7 1.5 collective-permute-start.7
  200.2 28.3 %collective-permute-done.7 = f32[2,2,632,128]{3,2,1,0:T(8,128)} collective-permute-done((f32[2,2,632,128]{3,2,1,0:T(8,128)S(1)}, f32[2,2,632,128]{3,2,1,0:T(8,128)}, u32[]{:S(2)}, u32[]{:S(2)}) %collective-permute-start.7) | collective-permute-done | bytes 1294368 | tf_op jit(solution)/shard_map/ppermute | solution.py:21
  228.6 1.8 fusion.12
  230.4 0.9 dynamic-slice_bitcast_fusion
  231.2 3.0 collective-permute-start.8
  234.2 13.8 %collective-permute-done.8 = f32[2,632,128]{2,1,0:T(8,128)} collective-permute-done((f32[2,632,128]{2,1,0:T(8,128)}, f32[2,632,128]{2,1,0:T(8,128)}, u32[]{:S(2)}, u32[]{:S(2)}) %collective-permute-start.8) | collective-permute-done | bytes 647200 | tf_op jit(solution)/shard_map/ppermute | solution.py:21
  248.0 1.2 bitcast_add_fusion.1
  249.2 6.1 %collective-permute-start.9 = (f32[632,128]{1,0:T(8,128)S(1)}, f32[632,128]{1,0:T(8,128)S(1)}, u32[]{:S(2)}, u32[]{:S(2)}) collective-permute-start(f32[632,128]{1,0:T(8,128)S(1)} %dynamic-slice_bitcast_fusion.1), channel_id=1, source_target_pairs={{0,1},{1,0},{2,3},{3,2},{4,5},{5,4},{6,7},{7,6},{8,9},{9,8},{10,11... | collective-permute-start | bytes 970760 | tf_op jit(solution)/shard_map/ppermute | solution.py:21
  255.4 2.0 convolution_convert_fusion
  257.4 12.4 %collective-permute-done.9 = f32[632,128]{1,0:T(8,128)S(1)} collective-permute-done((f32[632,128]{1,0:T(8,128)S(1)}, f32[632,128]{1,0:T(8,128)S(1)}, u32[]{:S(2)}, u32[]{:S(2)}) %collective-permute-start.9) | collective-permute-done | bytes 323616 | tf_op jit(solution)/shard_map/ppermute | solution.py:21
  270.7 7.5 %collective-permute-done.13 = f32[120,128]{1,0:T(8,128)S(1)} collective-permute-done((f32[120,128]{1,0:T(8,128)S(1)}, f32[120,128]{1,0:T(8,128)S(1)}, u32[]{:S(2)}, u32[]{:S(2)}) %collective-permute-start.13) | collective-permute-done | bytes 61472 | tf_op jit(solution)/shard_map/ppermute | solution.py:21
  278.4 5.1 %collective-permute-done.14 = f32[120,128]{1,0:T(8,128)S(1)} collective-permute-done((f32[120,128]{1,0:T(8,128)S(1)}, f32[120,128]{1,0:T(8,128)S(1)}, u32[]{:S(2)}, u32[]{:S(2)}) %collective-permute-start.14) | collective-permute-done | bytes 61472 | tf_op jit(solution)/shard_map/ppermute | solution.py:21
  283.7 2.9 collective-permute-start.11
  286.6 5.1 %collective-permute-done.15 = f32[120,128]{1,0:T(8,128)S(1)} collective-permute-done((f32[120,128]{1,0:T(8,128)S(1)}, f32[120,128]{1,0:T(8,128)S(1)}, u32[]{:S(2)}, u32[]{:S(2)}) %collective-permute-start.15) | collective-permute-done | bytes 61472 | tf_op jit(solution)/shard_map/ppermute | solution.py:21
  291.8 3.9 %collective-permute-start.16 = (f32[2,120,128]{2,1,0:T(8,128)S(1)}, f32[2,120,128]{2,1,0:T(8,128)S(1)}, u32[]{:S(2)}, u32[]{:S(2)}) collective-permute-start(f32[2,120,128]{2,1,0:T(8,128)S(1)} %maximum_select_fusion.8), channel_id=1, source_target_pairs={{0,4},{1,5},{2,6},{3,7},{4,0},{5,1},{6,2},{7,3},{8,12},{9,13},{10,... | collective-permute-start | bytes 368648 | tf_op jit(solution)/shard_map/ppermute | solution.py:21
  295.7 3.7 %collective-permute-done.16 = f32[2,120,128]{2,1,0:T(8,128)S(1)} collective-permute-done((f32[2,120,128]{2,1,0:T(8,128)S(1)}, f32[2,120,128]{2,1,0:T(8,128)S(1)}, u32[]{:S(2)}, u32[]{:S(2)}) %collective-permute-start.16) | collective-permute-done | bytes 122912 | tf_op jit(solution)/shard_map/ppermute | solution.py:21
  299.4 0.9 collective-permute-start.17
  300.4 1.3 collective-permute-start.12
  301.8 6.5 %collective-permute-done.17 = f32[2,2,120,128]{3,2,1,0:T(8,128)S(1)} collective-permute-done((f32[2,2,120,128]{3,2,1,0:T(8,128)S(1)}, f32[2,2,120,128]{3,2,1,0:T(8,128)S(1)}, u32[]{:S(2)}, u32[]{:S(2)}) %collective-permute-start.17) | collective-permute-done | bytes 245792 | tf_op jit(solution)/shard_map/ppermute | solution.py:21
  309.6 0.7 slice.51
  310.4 4.0 %collective-permute-done.12 = bf16[2,2,512,128]{3,2,1,0:T(8,128)(2,1)S(1)} collective-permute-done((bf16[2,2,512,128]{3,2,1,0:T(8,128)(2,1)S(1)}, bf16[2,2,512,128]{3,2,1,0:T(8,128)(2,1)S(1)}, u32[]{:S(2)}, u32[]{:S(2)}) %collective-permute-start.12) | collective-permute-done | bytes 524320 | tf_op jit(solution)/shard_map/ppermute | solution.py:21
  314.5 1.0 copy.26
  (92 shorter events, 4.9 us)
Async XLA Ops:
  0.6 33.6 %copy-start = (bf16[8192,128]{1,0:T(8,128)(2,1)S(1)}, bf16[8192,128]{1,0:T(8,128)(2,1)}, u32[]{:S(2)}) copy-start(bf16[8192,128]{1,0:T(8,128)(2,1)} %param.21) | copy-start | bytes 6291460
  1.5 9.2 %copy-start.19 = (s32[2048]{0:T(1024)S(1)}, s32[2048]{0:T(1024)}, u32[]{:S(2)}) copy-start(s32[2048]{0:T(1024)} %param.26) | copy-start | bytes 24580
  1.5 9.2 %copy-start.1 = (bf16[4096,128]{1,0:T(8,128)(2,1)S(1)}, bf16[4096,128]{1,0:T(8,128)(2,1)}, u32[]{:S(2)}) copy-start(bf16[4096,128]{1,0:T(8,128)(2,1)} %param.18) | copy-start | bytes 3145732
  10.7 26.2 %collective-permute-start.1 = (bf16[2048,128]{1,0:T(8,128)(2,1)}, bf16[2048,128]{1,0:T(8,128)(2,1)}, u32[]{:S(2)}, u32[]{:S(2)}) collective-permute-start(bf16[2048,128]{1,0:T(8,128)(2,1)} %gather_fusion.1), channel_id=1, source_target_pairs={{0,248},{8,0},{16,8},{24,16},{32,24},{40,32},{48,40},{56,48},{64,5... | collective-permute-start | bytes 1572872 | tf_op jit(solution)/shard_map/ppermute | solution.py:12
  10.7 8.6 %copy-start.14 = (bf16[128,128]{1,0:T(8,128)(2,1)S(1)}, bf16[128,128]{1,0:T(8,128)(2,1)}, u32[]{:S(2)}) copy-start(bf16[128,128]{1,0:T(8,128)(2,1)} %param.32) | copy-start | bytes 98308
  10.7 8.8 %copy-start.16 = (bf16[128,128]{1,0:T(8,128)(2,1)S(1)}, bf16[128,128]{1,0:T(8,128)(2,1)}, u32[]{:S(2)}) copy-start(bf16[128,128]{1,0:T(8,128)(2,1)} %param.33) | copy-start | bytes 98308
  10.7 8.8 %copy-start.21 = (f32[128]{0:T(128)S(1)}, f32[128]{0:T(128)}, u32[]{:S(2)}) copy-start(f32[128]{0:T(128)} %param.35) | copy-start | bytes 1540
  18.8 3.6 %copy-start.22 = (bf16[128,128]{1,0:T(8,128)(2,1)S(1)}, bf16[128,128]{1,0:T(8,128)(2,1)}, u32[]{:S(2)}) copy-start(bf16[128,128]{1,0:T(8,128)(2,1)} %param.34) | copy-start | bytes 98308
  18.8 18.1 %collective-permute-start = (bf16[2048,128]{1,0:T(8,128)(2,1)}, bf16[2048,128]{1,0:T(8,128)(2,1)}, u32[]{:S(2)}, u32[]{:S(2)}) collective-permute-start(bf16[2048,128]{1,0:T(8,128)(2,1)} %gather_fusion), channel_id=1, source_target_pairs={{0,8},{8,16},{16,24},{24,32},{32,40},{40,48},{48,56},{56,64},{64,7... | collective-permute-start | bytes 1572872 | tf_op jit(solution)/shard_map/ppermute | solution.py:12
  30.1 3.5 %copy-start.17 = (s32[8192]{0:T(1024)S(1)}, s32[8192]{0:T(1024)}, u32[]{:S(2)}) copy-start(s32[8192]{0:T(1024)} %param.23) | copy-start | bytes 98308
  30.1 4.1 %copy-start.12 = (bf16[128,128]{1,0:T(8,128)(2,1)S(1)}, bf16[128,128]{1,0:T(8,128)(2,1)}, u32[]{:S(2)}) copy-start(bf16[128,128]{1,0:T(8,128)(2,1)} %param.29) | copy-start | bytes 98308
  72.3 2.2 copy-start.5
  72.3 2.2 copy-start.11
  72.3 2.2 copy-start.20
  74.4 2.6 copy-start.8
  77.0 2.0 copy-start.23
  79.0 2.3 copy-start.6
  81.2 2.4 copy-start.2
  83.6 1.7 copy-start.9
  83.6 1.7 copy-start.10
  88.6 54.5 %collective-permute-start.4 = (f32[960,128]{1,0:T(8,128)S(1)}, f32[960,128]{1,0:T(8,128)}, u32[]{:S(2)}, u32[]{:S(2)}) collective-permute-start(f32[960,128]{1,0:T(8,128)S(1)} %pad.4), channel_id=1, source_target_pairs={{0,8},{8,0},{16,24},{24,16},{32,40},{40,32},{48,56},{56,48},{64,72... | collective-permute-start | bytes 1474568 | tf_op jit(solution)/shard_map/ppermute | solution.py:21
  144.2 15.1 %collective-permute-start.5 = (f32[960,128]{1,0:T(8,128)S(1)}, f32[960,128]{1,0:T(8,128)S(1)}, u32[]{:S(2)}, u32[]{:S(2)}) collective-permute-start(f32[960,128]{1,0:T(8,128)S(1)} %pad_add_fusion), channel_id=1, source_target_pairs={{0,16},{8,24},{16,0},{24,8},{32,48},{40,56},{48,32},{56,40},{64,80... | collective-permute-start | bytes 1474568 | tf_op jit(solution)/shard_map/ppermute | solution.py:21
  148.7 18.6 %collective-permute-start.2 = (bf16[2048,128]{1,0:T(8,128)(2,1)}, bf16[2048,128]{1,0:T(8,128)(2,1)}, u32[]{:S(2)}, u32[]{:S(2)}) collective-permute-start(bf16[2048,128]{1,0:T(8,128)(2,1)} %get-tuple-element.6), channel_id=1, source_target_pairs={{0,248},{8,0},{16,8},{24,16},{32,24},{40,32},{48,40},{56,48},{64,5... | collective-permute-start | bytes 1572872 | tf_op jit(solution)/shard_map/ppermute | solution.py:12
  151.0 30.0 %collective-permute-start.3 = (bf16[2048,128]{1,0:T(8,128)(2,1)}, bf16[2048,128]{1,0:T(8,128)(2,1)}, u32[]{:S(2)}, u32[]{:S(2)}) collective-permute-start(bf16[2048,128]{1,0:T(8,128)(2,1)} %get-tuple-element.5), channel_id=1, source_target_pairs={{0,8},{8,16},{16,24},{24,32},{32,40},{40,48},{48,56},{56,64},{64,7... | collective-permute-start | bytes 1572872 | tf_op jit(solution)/shard_map/ppermute | solution.py:12
  159.3 37.2 %collective-permute-start.6 = (f32[960,128]{1,0:T(8,128)S(1)}, f32[960,128]{1,0:T(8,128)S(1)}, u32[]{:S(2)}, u32[]{:S(2)}) collective-permute-start(f32[960,128]{1,0:T(8,128)S(1)} %add.152), channel_id=1, source_target_pairs={{0,32},{8,40},{16,48},{24,56},{32,0},{40,8},{48,16},{56,24},{64,96... | collective-permute-start | bytes 1474568 | tf_op jit(solution)/shard_map/ppermute | solution.py:21
  163.3 3.2 %copy-start.3 = (bf16[8192,128]{1,0:T(8,128)(2,1)S(1)}, bf16[8192,128]{1,0:T(8,128)(2,1)}, u32[]{:S(2)}) copy-start(bf16[8192,128]{1,0:T(8,128)(2,1)} %copy-done.2) | copy-start | bytes 6291460
  163.3 3.2 %copy-start.18 = (bf16[128,128]{1,0:T(8,128)(2,1)S(1)}, bf16[128,128]{1,0:T(8,128)(2,1)}, u32[]{:S(2)}) copy-start(bf16[128,128]{1,0:T(8,128)(2,1)} %param.27) | copy-start | bytes 98308
  167.3 27.3 %copy-start.15 = (bf16[128,128]{1,0:T(8,128)(2,1)S(1)}, bf16[128,128]{1,0:T(8,128)(2,1)}, u32[]{:S(2)}) copy-start(bf16[128,128]{1,0:T(8,128)(2,1)} %param.32) | copy-start | bytes 98308
  196.6 0.8 copy-start.7
  198.7 29.9 %collective-permute-start.7 = (f32[2,2,632,128]{3,2,1,0:T(8,128)S(1)}, f32[2,2,632,128]{3,2,1,0:T(8,128)}, u32[]{:S(2)}, u32[]{:S(2)}) collective-permute-start(f32[2,2,632,128]{3,2,1,0:T(8,128)S(1)} %fusion.9), channel_id=1, source_target_pairs={{0,2},{1,3},{2,0},{3,1},{4,6},{5,7},{6,4},{7,5},{8,10},{9,11},{10,... | collective-permute-start | bytes 3883016 | tf_op jit(solution)/shard_map/ppermute | solution.py:21
  230.3 25.0 %copy-start.13 = (bf16[128,128]{1,0:T(8,128)(2,1)S(1)}, bf16[128,128]{1,0:T(8,128)(2,1)}, u32[]{:S(2)}) copy-start(bf16[128,128]{1,0:T(8,128)(2,1)} %param.29) | copy-start | bytes 98308
  231.2 16.8 %collective-permute-start.8 = (f32[2,632,128]{2,1,0:T(8,128)}, f32[2,632,128]{2,1,0:T(8,128)}, u32[]{:S(2)}, u32[]{:S(2)}) collective-permute-start(f32[2,632,128]{2,1,0:T(8,128)} %dynamic-slice_bitcast_fusion), channel_id=1, source_target_pairs={{0,4},{1,5},{2,6},{3,7},{4,0},{5,1},{6,2},{7,3},{8,12},{9,13},{10,... | collective-permute-start | bytes 1941512 | tf_op jit(solution)/shard_map/ppermute | solution.py:21
  234.2 21.1 %copy-start.4 = (bf16[8192,128]{1,0:T(8,128)(2,1)S(1)}, bf16[8192,128]{1,0:T(8,128)(2,1)}, u32[]{:S(2)}) copy-start(bf16[8192,128]{1,0:T(8,128)(2,1)} %copy-done.2) | copy-start | bytes 6291460
  249.2 20.6 %collective-permute-start.9 = (f32[632,128]{1,0:T(8,128)S(1)}, f32[632,128]{1,0:T(8,128)S(1)}, u32[]{:S(2)}, u32[]{:S(2)}) collective-permute-start(f32[632,128]{1,0:T(8,128)S(1)} %dynamic-slice_bitcast_fusion.1), channel_id=1, source_target_pairs={{0,1},{1,0},{2,3},{3,2},{4,5},{5,4},{6,7},{7,6},{8,9},{9,8},{10,11... | collective-permute-start | bytes 970760 | tf_op jit(solution)/shard_map/ppermute | solution.py:21
  269.9 8.4 %collective-permute-start.13 = (f32[120,128]{1,0:T(8,128)S(1)}, f32[120,128]{1,0:T(8,128)S(1)}, u32[]{:S(2)}, u32[]{:S(2)}) collective-permute-start(f32[120,128]{1,0:T(8,128)S(1)} %slice.49), channel_id=1, source_target_pairs={{0,64},{8,72},{16,80},{24,88},{32,96},{40,104},{48,112},{56,120},{... | collective-permute-start | bytes 184328 | tf_op jit(solution)/shard_map/ppermute | solution.py:21
  270.1 13.6 %collective-permute-start.10 = (bf16[512,128]{1,0:T(8,128)(2,1)S(1)}, bf16[512,128]{1,0:T(8,128)(2,1)S(1)}, u32[]{:S(2)}, u32[]{:S(2)}) collective-permute-start(bf16[512,128]{1,0:T(8,128)(2,1)S(1)} %slice.57), channel_id=1, source_target_pairs={{0,1},{1,0},{2,3},{3,2},{4,5},{5,4},{6,7},{7,6},{8,9},{9,8},{10,11... | collective-permute-start | bytes 393224 | tf_op jit(solution)/shard_map/ppermute | solution.py:21
  278.3 5.2 %collective-permute-start.14 = (f32[120,128]{1,0:T(8,128)S(1)}, f32[120,128]{1,0:T(8,128)S(1)}, u32[]{:S(2)}, u32[]{:S(2)}) collective-permute-start(f32[120,128]{1,0:T(8,128)S(1)} %slice_add_fusion), channel_id=1, source_target_pairs={{0,128},{8,136},{16,144},{24,152},{32,160},{40,168},{48,176},{56,1... | collective-permute-start | bytes 184328 | tf_op jit(solution)/shard_map/ppermute | solution.py:21
  283.5 8.3 %collective-permute-start.15 = (f32[120,128]{1,0:T(8,128)S(1)}, f32[120,128]{1,0:T(8,128)S(1)}, u32[]{:S(2)}, u32[]{:S(2)}) collective-permute-start(f32[120,128]{1,0:T(8,128)S(1)} %add.164), channel_id=1, source_target_pairs={{0,1},{1,0},{2,3},{3,2},{4,5},{5,4},{6,7},{7,6},{8,9},{9,8},{10,11... | collective-permute-start | bytes 184328 | tf_op jit(solution)/shard_map/ppermute | solution.py:21
  283.7 16.7 %collective-permute-start.11 = (bf16[2,512,128]{2,1,0:T(8,128)(2,1)S(1)}, bf16[2,512,128]{2,1,0:T(8,128)(2,1)S(1)}, u32[]{:S(2)}, u32[]{:S(2)}) collective-permute-start(bf16[2,512,128]{2,1,0:T(8,128)(2,1)S(1)} %maximum_select_fusion.5), channel_id=1, source_target_pairs={{0,4},{1,5},{2,6},{3,7},{4,0},{5,1},{6,2},{7,3},{8,12},{9,13},{10,... | collective-permute-start | bytes 786440 | tf_op jit(solution)/shard_map/ppermute | solution.py:21
  291.8 7.6 %collective-permute-start.16 = (f32[2,120,128]{2,1,0:T(8,128)S(1)}, f32[2,120,128]{2,1,0:T(8,128)S(1)}, u32[]{:S(2)}, u32[]{:S(2)}) collective-permute-start(f32[2,120,128]{2,1,0:T(8,128)S(1)} %maximum_select_fusion.8), channel_id=1, source_target_pairs={{0,4},{1,5},{2,6},{3,7},{4,0},{5,1},{6,2},{7,3},{8,12},{9,13},{10,... | collective-permute-start | bytes 368648 | tf_op jit(solution)/shard_map/ppermute | solution.py:21
  299.4 8.9 %collective-permute-start.17 = (f32[2,2,120,128]{3,2,1,0:T(8,128)S(1)}, f32[2,2,120,128]{3,2,1,0:T(8,128)S(1)}, u32[]{:S(2)}, u32[]{:S(2)}) collective-permute-start(f32[2,2,120,128]{3,2,1,0:T(8,128)S(1)} %maximum_select_fusion.6), channel_id=1, source_target_pairs={{0,2},{1,3},{2,0},{3,1},{4,6},{5,7},{6,4},{7,5},{8,10},{9,11},{10,... | collective-permute-start | bytes 737288 | tf_op jit(solution)/shard_map/ppermute | solution.py:21
  300.4 13.9 %collective-permute-start.12 = (bf16[2,2,512,128]{3,2,1,0:T(8,128)(2,1)S(1)}, bf16[2,2,512,128]{3,2,1,0:T(8,128)(2,1)S(1)}, u32[]{:S(2)}, u32[]{:S(2)}) collective-permute-start(bf16[2,2,512,128]{3,2,1,0:T(8,128)(2,1)S(1)} %maximum_select_fusion.2), channel_id=1, source_target_pairs={{0,2},{1,3},{2,0},{3,1},{4,6},{5,7},{6,4},{7,5},{8,10},{9,11},{10,... | collective-permute-start | bytes 1572872 | tf_op jit(solution)/shard_map/ppermute | solution.py:21
